TPU v7x, 32 devices: a whole 2x2x4 slice. The times are simulated.
32 devices in a mesh: dp: 8 (over y, x, core), tensor: 4 (over z).
Axes of the slice: x: 2, y: 2, z: 4, core: 2. Of those that a mesh axis runs over, the one named last changes fastest.
Arguments:
- queries: bfloat16 [256, 32, 16384], P('dp', None, 'tensor'), may hold values from -6 to 6
- key_rows: bfloat16 [256, 32, 1024], P(('dp', 'tensor')), may hold values from -6 to 6
- value_rows: bfloat16 [256, 32, 1024], P(('dp', 'tensor')), may hold values from -6 to 6
- destination: int32 [256], P('dp'), may hold values from 0 to 7, as said below
- token_count: int32 [256], P('dp'), may hold values from 16 to 32, as said below
- doc_ids: int32 [8, 1024], P('dp'), may hold values from 0 to 7, never falling along the last dimension, each value on 1 to 256 neighbouring positions
Outputs:
- attended: bfloat16 [8192, 16384], P('dp', 'tensor')
Inputs may be any that keep to these rules, and one draw needn't show every extreme that they name: `destination`: every data group is named by exactly 32 sentences; of the 32 sentences of one group at most 8 name the same group, and some group sends exactly 8 sentences to one group in every draw. `token_count`: in every draw some data group receives only sentences with 32 live tokens, so its total is 1024.
All inputs are finite; a program needn't handle non-finite values.
Results may differ from a plain program's by a relative error of at most 0.0034.
Values may be sent and summed in bfloat16 or wider, within the bound.
A program may use at most 256 MiB of HBM per device.

v0:
```python
import jax
import jax.numpy as jnp
from jax import lax
from jax.sharding import PartitionSpec as P

HEAD_DIM = 128


def per_device(queries, key_rows, value_rows, destination, token_count, doc_ids):
    groups = lax.axis_size("dp")
    own_group = lax.axis_index("dp")
    sentences = destination.shape[0]
    slot_len = queries.shape[1]
    capacity = max(2, (2 * sentences + groups - 1) // groups)
    every_dest, every_count = (
        lax.all_gather(destination, "dp", axis=0, tiled=True),
        lax.all_gather(token_count, "dp", axis=0, tiled=True),
    )
    all_keys, all_values = (
        lax.all_gather(key_rows, "tensor", axis=0, tiled=True),
        lax.all_gather(value_rows, "tensor", axis=0, tiled=True),
    )
    kv_width = all_keys.shape[2] // lax.axis_size("tensor")
    kv_start = lax.axis_index("tensor") * kv_width
    head_keys = lax.dynamic_slice_in_dim(all_keys, kv_start, kv_width, 2)
    head_values = lax.dynamic_slice_in_dim(all_values, kv_start, kv_width, 2)
    order = jnp.arange(sentences, dtype=jnp.int32)
    same_dest = destination[:, None] == destination[None, :]
    earlier = order[None, :] < order[:, None]
    rank_in = jnp.sum((same_dest & earlier).astype(jnp.int32), axis=1)
    target = destination * capacity + rank_in
    buckets = jnp.arange(groups * capacity, dtype=jnp.int32)
    matches = target[None, :] == buckets[:, None]
    filled = jnp.any(matches, axis=1)
    picked = jnp.sum(jnp.where(matches, order[None, :], 0), axis=1)

    def bucket_rows(rows):
        taken = jnp.take(rows, picked, axis=0)
        return jnp.where(filled[:, None, None], taken, jnp.zeros_like(taken))

    got_q, got_k, got_v = (
        lax.all_to_all(bucket_rows(queries), "dp", split_axis=0, concat_axis=0, tiled=True),
        lax.all_to_all(bucket_rows(head_keys), "dp", split_axis=0, concat_axis=0, tiled=True),
        lax.all_to_all(bucket_rows(head_values), "dp", split_axis=0, concat_axis=0, tiled=True),
    )
    table_dest = every_dest.reshape(groups, sentences)
    table_count = every_count.reshape(groups, sentences)
    mine = (table_dest == own_group).astype(jnp.int32)
    place_rank = jnp.cumsum(mine, axis=1) - mine
    slot_ids = jnp.arange(capacity, dtype=jnp.int32)
    hits = (mine[:, :, None] == 1) & (place_rank[:, :, None] == slot_ids[None, None, :])
    sizes = jnp.sum(jnp.where(hits, table_count[:, :, None], 0), axis=1).reshape(groups * capacity)
    ends = jnp.cumsum(sizes)
    starts = ends - sizes
    total = ends[-1]
    row_len = doc_ids.shape[1]
    place = jnp.arange(row_len, dtype=jnp.int32)
    which = jnp.sum((place[:, None] >= ends[None, :]).astype(jnp.int32), axis=1)
    which = jnp.minimum(which, groups * capacity - 1)
    owner = which[:, None] == buckets[None, :]
    offset = jnp.clip(
        place - jnp.sum(jnp.where(owner, starts[None, :], 0), axis=1), 0, slot_len - 1
    )
    flat_index = which * slot_len + offset
    packed_q = jnp.take(got_q.reshape(-1, got_q.shape[2]), flat_index, axis=0)
    packed_k = jnp.take(got_k.reshape(-1, got_k.shape[2]), flat_index, axis=0)
    packed_v = jnp.take(got_v.reshape(-1, got_v.shape[2]), flat_index, axis=0)
    kv_local = packed_k.shape[1] // HEAD_DIM
    q_local = packed_q.shape[1] // HEAD_DIM
    per_group = q_local // kv_local
    scale_factor = HEAD_DIM ** (-0.5)
    block = 512
    tile_count = row_len // block
    docs = doc_ids[0]
    pieces = []
    for q_tile_idx in range(tile_count):
        q_begin = q_tile_idx * block
        q_tile = packed_q[q_begin : q_begin + block].reshape(block, kv_local, per_group, HEAD_DIM)
        rows = q_begin + jnp.arange(block, dtype=jnp.int32)
        row_docs = docs[q_begin : q_begin + block]

        def score_only(k_tile_idx, q_tile=q_tile):
            k_begin = k_tile_idx * block
            k_tile = packed_k[k_begin : k_begin + block].reshape(block, kv_local, HEAD_DIM)
            return (
                jnp.einsum("qkgd,skd->kgqs", q_tile, k_tile, preferred_element_type=jnp.float32)
                * scale_factor
            )

        def mask_of(k_tile_idx, rows=rows, row_docs=row_docs):
            k_begin = k_tile_idx * block
            cols = k_begin + jnp.arange(block, dtype=jnp.int32)
            return (
                (cols[None, :] <= rows[:, None])
                & (docs[k_begin : k_begin + block][None, :] == row_docs[:, None])
                & (rows[:, None] < total)
            )

        peak_val = jnp.full((kv_local, per_group, block), -1e30, jnp.float32)
        kept = []
        for k_tile_idx in range(q_tile_idx + 1):
            scores = score_only(k_tile_idx)
            allowed = mask_of(k_tile_idx)
            kept.append((scores, allowed))
            peak_val = jnp.maximum(
                peak_val, jnp.max(jnp.where(allowed[None, None], scores, -1e30), axis=3)
            )
        carry = (
            jnp.zeros((kv_local, per_group, block), jnp.float32),
            jnp.zeros((kv_local, per_group, block, HEAD_DIM), jnp.float32),
        )
        for k_tile_idx in range(q_tile_idx + 1):
            scores, allowed = kept[k_tile_idx]
            add_norm_sum, add_accum = carry
            weight = jnp.where(allowed[None, None], jnp.exp(scores - peak_val[..., None]), 0.0)
            add_k_begin = k_tile_idx * block
            v_tile = packed_v[add_k_begin : add_k_begin + block].reshape(block, kv_local, HEAD_DIM)
            mixed = jnp.einsum(
                "kgqs,skd->kgqd",
                weight.astype(jnp.bfloat16),
                v_tile,
                preferred_element_type=jnp.float32,
            )
            carry = (add_norm_sum + jnp.sum(weight, axis=3), add_accum + mixed)
        norm_sum, accum = carry
        result = accum / jnp.where(norm_sum > 0, norm_sum, 1.0)[..., None]
        result = jnp.where((norm_sum > 0)[..., None], result, 0.0)
        result = jnp.transpose(result, (2, 0, 1, 3)).reshape(block, q_local * HEAD_DIM)
        pieces.append(result.astype(jnp.bfloat16))
    return jnp.concatenate(pieces, axis=0)


def solution(mesh):
    placed = (
        P("dp", None, "tensor"),
        P(("dp", "tensor"), None, None),
        P(("dp", "tensor"), None, None),
        P("dp"),
        P("dp"),
        P("dp", None),
    )
    return jax.shard_map(
        per_device, mesh=mesh, in_specs=placed, out_specs=P("dp", "tensor"), check_vma=False
    )
```

profile of v0, /device:TPU:0, one launch (start us, length us, event | category | flops | bytes accessed | tf_op | source)
XLA Modules:
  0.0 563.0 jit_solution(17614540362025320532)
XLA Ops:
  9.8 47.8 %all-gather.5.cloned.1.call-done = bf16[32,32,1024]{2,1,0:T(8,128)(2,1)} async-done(((bf16[8,32,1024]{2,1,0:T(8,128)(2,1)}), bf16[32,32,1024]{2,1,0:T(8,128)(2,1)}) %all-gather.5.cloned.1.call-update) | async-done | bytes 2097168 | tf_op jit(solution)/shard_map/all_gather | solution.py:21
  57.6 1.1 constant_dynamic-slice_fusion
  59.3 44.6 %all-gather.3.cloned.1.call-done = bf16[32,32,1024]{2,1,0:T(8,128)(2,1)} async-done(((bf16[8,32,1024]{2,1,0:T(8,128)(2,1)}), bf16[32,32,1024]{2,1,0:T(8,128)(2,1)}) %all-gather.3.cloned.1.call-update) | async-done | bytes 2097168 | tf_op jit(solution)/shard_map/all_gather | solution.py:20
  103.9 1.1 constant_dynamic-slice_fusion.1
  105.6 1.7 select_select_fusion.2
  107.2 3.6 all-to-all-start.2
  110.9 10.8 %gather_fusion = bf16[64,32,4096]{2,1,0:T(8,128)(2,1)} fusion(bf16[32,32,4096]{2,1,0:T(8,128)(2,1)} %param.10, s32[1024]{0:T(1024)S(1)} %pad_clamp_fusion), kind=kCustom, calls=%fused_computation.4 | custom fusion | bytes 33554688 | tf_op jit(solution)/shard_map/jit(_take)/gather | solution.py:38
  121.6 4.6 all-to-all-done.2
  126.3 3.6 all-to-all-start
  129.8 14.3 %select_select_fusion = bf16[64,32,4096]{2,1,0:T(8,128)(2,1)} fusion(bf16[64,32,4096]{2,1,0:T(8,128)(2,1)} %gather_fusion, pred[64]{0:T(512)(128)(4,1)S(1)} %compare_and_fusion.1, pred[64]{0:T(512)(128)(4,1)S(1)} %fusion.37), kind=kLoop, calls=%fused_computation.27 | loop fusion | flops 16777216 | bytes 33554560 | tf_op jit(solution)/shard_map/jit(_where)/select_n | solution.py:39
  144.2 1.0 all-to-all-done
  145.2 5.8 %all-to-all-start.1 = ((bf16[64,32,4096]{2,1,0:T(8,128)(2,1)}), bf16[64,32,4096]{2,1,0:T(8,128)(2,1)}, u32[]{:S(2)}, u32[]{:S(2)}) async-start(bf16[64,32,4096]{2,1,0:T(8,128)(2,1)} %select_select_fusion), calls=%async_computation.1 | async-start | bytes 33554432 | tf_op jit(solution)/shard_map/all_to_all | solution.py:42
  152.7 184.3 %all-reduce.2 = (s32[256]{0:T(256)S(1)}, s32[256]{0:T(256)S(1)}) all-reduce(s32[256]{0:T(256)S(1)} %dynamic-update-slice.1, s32[256]{0:T(256)S(1)} %dynamic-update-slice), channel_id=1, replica_groups=mesh['dp'=8,'tensor'=4] {'dp'}, use_global_device_ids=true, to_apply=%add.1 | all-reduce | flops 512 | bytes 4096
  339.5 1.1 fusion.35
  340.6 3.9 gather_fusion.5
  344.6 3.9 gather_fusion.3
  349.4 23.0 %gather_fusion.1 = bf16[1024,4096]{1,0:T(8,128)(2,1)} fusion(bf16[2048,4096]{1,0:T(8,128)(2,1)} %bitcast.8, s32[1024]{0:T(1024)S(1)} %broadcast_clamp_fusion), kind=kCustom, calls=%fused_computation.5 | custom fusion | bytes 16781312 | tf_op jit(solution)/shard_map/jit(_take)/gather | solution.py:65
  372.4 7.6 %broadcast_select_fusion = bf16[1024,4096]{1,0:T(8,128)(2,1)} fusion(bf16[1024,4096]{1,0:T(8,128)(2,1)} %gather_fusion.1, pred[1024]{0:T(1024)(128)(4,1)S(1)} %compare_and_fusion), kind=kLoop, calls=%fused_computation.41 | loop fusion | flops 4194304 | bytes 16778240 | tf_op jit(solution)/shard_map/jit(_take)/select_n | solution.py:65
  380.0 5.9 %fusion.46 = (bf16[512,4096]{1,0:T(8,128)(2,1)}, bf16[512,4096]{1,0:T(8,128)(2,1)}) fusion(bf16[1024,4096]{1,0:T(8,128)(2,1)} %broadcast_select_fusion), kind=kLoop, calls=%fused_computation.99 | loop fusion | bytes 16777216 | tf_op jit(solution)/shard_map/slice | solution.py:78
  385.9 6.4 %copy.53 = bf16[512,4096]{0,1:T(8,128)(2,1)} copy(bf16[512,4096]{1,0:T(8,128)(2,1)} %get-tuple-element.11) | data formatting | bytes 8388608 | tf_op jit(solution)/shard_map/slice | solution.py:78
  392.3 15.8 %fusion.6 = (f32[2,16,512]{2,1,0:T(8,128)S(1)}, f32[2,512,512,16]{2,1,3,0:T(8,128)}) fusion(pred[512,512]{0,1:T(8,128)(4,1)S(1)} %get-tuple-element.23, bf16[512,2,128,1]{0,2,3,1:T(8,128)(2,1)S(1)} %bitcast.123, bf16[512,2,16,128]{0,3,2,1:T(8,128)(2,1)} %bitcast.118), kind=kOutput, calls=%fused_computation.18 | convolution fusion | flops 2172633088 | bytes 38338560 | tf_op jit(solution)/shard_map/qkgd,skd->kgqs/dot_general | solution.py:86
  408.2 14.5 %fusion.10 = f32[2,16,512]{2,1,0:T(8,128)S(1)} fusion(f32[2,512,512,16]{2,1,3,0:T(8,128)} %get-tuple-element.33, f32[2,16,512]{2,1,0:T(8,128)S(1)} %broadcast_maximum_fusion, pred[512,512]{0,1:T(8,128)(4,1)S(1)} %get-tuple-element.23), kind=kLoop, calls=%fused_computation.22 | loop fusion | flops 33538048 | bytes 33947648 | tf_op jit(solution)/shard_map/reduce_sum | solution.py:124
  422.7 6.4 %copy.58 = bf16[512,4096]{0,1:T(8,128)(2,1)} copy(bf16[512,4096]{1,0:T(8,128)(2,1)} %get-tuple-element.12) | data formatting | bytes 8388608 | tf_op jit(solution)/shard_map/slice | solution.py:78
  429.1 16.2 %fusion.3 = (f32[2,16,512]{2,1,0:T(8,128)S(1)}, f32[2,512,512,16]{2,1,3,0:T(8,128)}) fusion(pred[512,512]{0,1:T(8,128)(4,1)S(1)} %get-tuple-element.17, bf16[512,2,128,1]{0,2,3,1:T(8,128)(2,1)S(1)} %bitcast.124, bf16[512,2,16,128]{0,3,2,1:T(8,128)(2,1)} %bitcast.116), kind=kOutput, calls=%fused_computation.13 | convolution fusion | flops 2172633088 | bytes 38338560 | tf_op jit(solution)/shard_map/qkgd,skd->kgqs/dot_general | solution.py:86
  445.3 13.9 %fusion = (f32[2,16,512]{2,1,0:T(8,128)S(1)}, f32[2,512,512,16]{2,1,3,0:T(8,128)}) fusion(pred[512,512]{0,1:T(8,128)(4,1)S(1)} %get-tuple-element.18, bf16[512,2,128,1]{0,2,3,1:T(8,128)(2,1)S(1)} %bitcast.125, bf16[512,2,16,128]{0,3,2,1:T(8,128)(2,1)S(1)} %bitcast.117), kind=kOutput, calls=%fused_computation.8 | convolution fusion | flops 2172633088 | bytes 38338560 | tf_op jit(solution)/shard_map/qkgd,skd->kgqs/dot_general | solution.py:86
  459.3 24.4 %fusion.14 = (f32[2,16,512]{2,1,0:T(8,128)S(1)}, f32[2,16,512]{2,1,0:T(8,128)S(1)}) fusion(f32[2,512,512,16]{2,1,3,0:T(8,128)} %get-tuple-element.29, f32[2,16,512]{2,1,0:T(8,128)S(1)} %maximum_maximum_fusion, pred[512,512]{0,1:T(8,128)(4,1)S(1)} %get-tuple-element.18, f32[2,512,512,16]{2,1,3,0:T(8,128)} %get-tuple-element.31, ...), kind=kLoop, calls=%fused_computation.26 | loop fusion | flops 67076096 | bytes 67829760 | tf_op jit(solution)/shard_map/reduce_sum | solution.py:124
  483.7 15.7 %fusion.27 = bf16[512,2,16,128]{0,3,2,1:T(8,128)(2,1)} fusion(f32[512,2,16]{0,2,1:T(8,128)S(1)} %bitcast_select_fusion.4, pred[512,2,16]{0,2,1:T(8,128)(4,1)S(1)} %bitcast_compare_fusion.1, bf16[512,2,128,1]{0,2,3,1:T(8,128)(2,1)S(1)} %bitcast.126, f32[2,512,512,16]{2,1,3,0:T(8,128)} %get-tuple-element.33, f32[2,16,512]{2,1,0:T(8,128)S(1)} %broadcast_maximum_fusion, ...), kind=kOutput, calls=%fused_computation.40 | convolution fusion | flops 2187329536 | bytes 38420480 | tf_op jit(solution)/shard_map/kgqs,skd->kgqd/dot_general | solution.py:118
  499.4 6.4 %copy.67 = bf16[512,4096]{1,0:T(8,128)(2,1)} copy(bf16[512,4096]{0,1:T(8,128)(2,1)} %bitcast.122) | data formatting | bytes 8388608 | tf_op jit(solution)/shard_map/convert_element_type | solution.py:129
  505.9 16.9 %fusion.15 = f32[2,16,512,128]{2,3,1,0:T(8,128)} fusion(bf16[512,2,128,1]{0,2,3,1:T(8,128)(2,1)S(1)} %bitcast.128, f32[2,512,512,16]{2,1,3,0:T(8,128)} %get-tuple-element.29, f32[2,16,512]{2,1,0:T(8,128)S(1)} %maximum_maximum_fusion, pred[512,512]{0,1:T(8,128)(4,1)S(1)} %get-tuple-element.18), kind=kOutput, calls=%fused_computation.28 | convolution fusion | flops 2181038080 | bytes 42532864 | tf_op jit(solution)/shard_map/kgqs,skd->kgqd/dot_general | solution.py:118
  522.8 18.9 %fusion.25 = bf16[512,2,16,128]{0,3,2,1:T(8,128)(2,1)} fusion(f32[2,16,512,128]{2,3,1,0:T(8,128)} %fusion.15, f32[512,2,16]{0,2,1:T(8,128)S(1)} %bitcast_select_fusion.3, pred[512,2,16]{0,2,1:T(8,128)(4,1)S(1)} %bitcast_compare_fusion, bf16[512,2,128,1]{0,2,3,1:T(8,128)(2,1)S(1)} %bitcast.127, f32[2,512,512,16]{2,1,3,0:T(8,128)} %get-tuple-element.31, ...), kind=kOutput, calls=%fused_computation.37 | convolution fusion | flops 2189426688 | bytes 46809088 | tf_op jit(solution)/shard_map/kgqs,skd->kgqd/dot_general | solution.py:118
  541.8 6.4 %copy.68 = bf16[512,4096]{1,0:T(8,128)(2,1)} copy(bf16[512,4096]{0,1:T(8,128)(2,1)} %bitcast.121) | data formatting | bytes 8388608 | tf_op jit(solution)/shard_map/convert_element_type | solution.py:129
  548.2 8.0 %pad_maximum_fusion = bf16[1024,4096]{1,0:T(8,128)(2,1)} fusion(bf16[512,4096]{1,0:T(8,128)(2,1)} %copy.68, bf16[512,4096]{1,0:T(8,128)(2,1)} %copy.67), kind=kLoop, calls=%fused_computation.34 | loop fusion | flops 16777216 | bytes 16777216 | tf_op jit(solution)/shard_map/concatenate | solution.py:130
  (66 shorter events, 8.8 us)
Async XLA Ops:
  6.5 51.1 %all-gather.5.cloned.1.call-start = ((), (), s32[]{:S(2)}) async-start(), calls=%async_computation.4 | async-start | bytes 2621440 | tf_op jit(solution)/shard_map/all_gather | solution.py:21
  7.3 96.6 %all-gather.3.cloned.1.call-start = ((), (), s32[]{:S(2)}) async-start(), calls=%async_computation.3 | async-start | bytes 2621440 | tf_op jit(solution)/shard_map/all_gather | solution.py:20
  107.2 19.0 %all-to-all-start.2 = ((bf16[64,32,256]{2,1,0:T(8,128)(2,1)}), bf16[64,32,256]{2,1,0:T(8,128)(2,1)S(1)}, u32[]{:S(2)}, u32[]{:S(2)}) async-start(bf16[64,32,256]{2,1,0:T(8,128)(2,1)} %get-tuple-element.27), calls=%async_computation.2 | async-start | bytes 2097152 | tf_op jit(solution)/shard_map/all_to_all | solution.py:44
  126.3 18.9 %all-to-all-start = ((bf16[64,32,256]{2,1,0:T(8,128)(2,1)}), bf16[64,32,256]{2,1,0:T(8,128)(2,1)S(1)}, u32[]{:S(2)}, u32[]{:S(2)}) async-start(bf16[64,32,256]{2,1,0:T(8,128)(2,1)} %get-tuple-element.26), calls=%async_computation | async-start | bytes 2097152 | tf_op jit(solution)/shard_map/all_to_all | solution.py:43
  144.2 6.8 %copy-start.4 = (u32[32]{0:T(128)S(1)}, u32[32]{0:T(128)}, u32[]{:S(2)}) copy-start(u32[32]{0:T(128)} %constant.102) | copy-start | bytes 388
  144.2 8.0 %copy-start.2 = (s32[32]{0:T(128)S(1)}, s32[32]{0:T(128)}, u32[]{:S(2)}) copy-start(s32[32]{0:T(128)} %param.13) | copy-start | bytes 388
  144.2 8.3 %copy-start.3 = (s32[32]{0:T(128)S(1)}, s32[32]{0:T(128)}, u32[]{:S(2)}) copy-start(s32[32]{0:T(128)} %param.14) | copy-start | bytes 388
  144.2 195.2 %copy-start.1 = (s32[1,1024]{1,0:T(1,128)S(1)}, s32[1,1024]{1,0:T(1,128)}, u32[]{:S(2)}) copy-start(s32[1,1024]{1,0:T(1,128)} %param.15) | copy-start | bytes 12292
  145.2 204.3 %all-to-all-start.1 = ((bf16[64,32,4096]{2,1,0:T(8,128)(2,1)}), bf16[64,32,4096]{2,1,0:T(8,128)(2,1)}, u32[]{:S(2)}, u32[]{:S(2)}) async-start(bf16[64,32,4096]{2,1,0:T(8,128)(2,1)} %select_select_fusion), calls=%async_computation.1 | async-start | bytes 33554432 | tf_op jit(solution)/shard_map/all_to_all | solution.py:42
  429.1 16.2 %copy-start = (bf16[512,4096]{0,1:T(8,128)(2,1)S(1)}, bf16[512,4096]{0,1:T(8,128)(2,1)}, u32[]{:S(2)}) copy-start(bf16[512,4096]{0,1:T(8,128)(2,1)} %copy.58) | copy-start | bytes 12582916
Sparse Core Ops, SparseCore 0:
  8.9 48.6 all-gather.4
  59.2 44.6 all-gather.2
where the time goes:
time: 564 us; the launch traced here: 563 us
  blocking collectives  184 us (33%)
  waiting for transfers between devices  99.4 us (18%)
  matrix products  97.6 us (17%)
  local copies, waits for them, and re-layouts  79.1 us (14%)
  other arithmetic  75.2 us (13%)
  between operations  14.4 us (3%)
  starting transfers between devices  13 us (2%)
    unnamed x1, blocking collectives  184 us
    dot_general x3, matrix products, per_device(): jnp.einsum('kgqs,skd->kgqd', weight.astype(jnp.bfloat16), v_tile, preferr...  51.6 us
    all_gather x1, waiting for transfers between devices, per_device(): lax.all_gather(value_rows, 'tensor', axis=0, tiled=True)  47.8 us
    dot_general x3, matrix products, score_only(): jnp.einsum('qkgd,skd->kgqs', q_tile, k_tile, preferred_element_type=jnp.f...  46 us
    all_gather x1, waiting for transfers between devices, per_device(): lax.all_gather(key_rows, 'tensor', axis=0, tiled=True)  44.6 us
    reduce_sum x2, other arithmetic, per_device(): carry = (add_norm_sum + jnp.sum(weight, axis=3), add_accum + mixed)  38.9 us
    gather x1, local copies, waits for them, and re-layouts, per_device(): packed_q = jnp.take(got_q.reshape(-1, got_q.shape[2]), flat_index, axis=0)  23 us
    slice x3, local copies, waits for them, and re-layouts, per_device(): packed_q[q_begin:q_begin + block]  18.7 us
  transfers between devices with their start and end apart: 5, of which 4 were waited for; matrix products, arithmetic and copies ran while one was open for 7% of the time, Pallas kernels for 0%

commit v1 on v0

v1 whole, which is shorter than its diff:
```python
import functools
import jax
import jax.numpy as jnp
from jax import lax
from jax.experimental import pallas as pl
from jax.experimental.pallas import tpu as pltpu
from jax.sharding import PartitionSpec as P

HEAD_DIM = 128
DOC_MAX = 256
LEAST = 16
TILE = 128
CHUNK_HEADS = 8
NEG = -1e30
LOG2E = 1.4426950408889634


def bucket_kernel(target_ref, rows_ref, out_ref, sem, *, col, width):
    count = target_ref.shape[0]

    for s in range(count):
        pltpu.make_async_copy(
            rows_ref.at[s, :, pl.ds(col, width)], out_ref.at[target_ref[s]], sem
        ).start()
    pltpu.make_async_copy(
        rows_ref.at[:, :, pl.ds(col, width)], out_ref.at[pl.ds(0, count)], sem
    ).wait()


def bucket(rows, target, slots, col, width):
    return pl.pallas_call(
        functools.partial(bucket_kernel, col=col, width=width),
        grid_spec=pltpu.PrefetchScalarGridSpec(
            num_scalar_prefetch=1,
            grid=(1,),
            in_specs=[pl.BlockSpec(memory_space=pl.ANY)],
            out_specs=pl.BlockSpec(memory_space=pl.ANY),
            scratch_shapes=[pltpu.SemaphoreType.DMA],
        ),
        out_shape=jax.ShapeDtypeStruct((slots, rows.shape[1], width), rows.dtype),
        cost_estimate=pl.CostEstimate(
            flops=0, transcendentals=0, bytes_accessed=4 * rows.shape[0] * rows.shape[1] * width
        ),
        name="bucket",
    )(target, rows)


def attend_kernel(
    slot_ref, first_ref, q_ref, kv_ref, pick_ref, bias_ref, *rest, kv_head, kv_width, heads, span
):
    out_ref, q_buf, kv_buf, k_pad, v_pad, sem_q, sem_kv = rest[-7:]
    tile = pl.program_id(0)
    sentences, slot_len, window = slot_ref.shape[0], q_ref.shape[1], pick_ref.shape[1]
    tiles = pl.num_programs(0)

    @pl.when(tile == 0)
    def _():
        for k in range(sentences):
            slot = slot_ref[k]
            rows = pl.ds(k * slot_len, slot_len)
            pltpu.make_async_copy(kv_ref.at[slot], kv_buf.at[rows], sem_kv).start()
            pltpu.make_async_copy(q_ref.at[slot], q_buf.at[rows], sem_q).start()
        pltpu.make_async_copy(kv_buf, kv_buf, sem_kv).wait()
        k_pad[:DOC_MAX] = jnp.zeros((DOC_MAX, HEAD_DIM), jnp.bfloat16)
        v_pad[:DOC_MAX] = jnp.zeros((DOC_MAX, HEAD_DIM), jnp.bfloat16)

        @pl.loop(0, tiles)
        def _(t):
            begin = pl.multiple_of(first_ref[t] * slot_len, slot_len)
            here = pl.multiple_of(t * TILE, TILE)
            pick = pick_ref[pl.ds(here, TILE), :]
            for pad, col in ((k_pad, kv_head * HEAD_DIM), (v_pad, kv_width + kv_head * HEAD_DIM)):
                piece = kv_buf[pl.ds(begin, window), col : col + HEAD_DIM]
                pad[pl.ds(DOC_MAX + here, TILE), :] = jnp.dot(
                    pick, piece, preferred_element_type=jnp.float32
                ).astype(jnp.bfloat16)

        pltpu.make_async_copy(q_buf, q_buf, sem_q).wait()

    here = pl.multiple_of(tile * TILE, TILE)
    begin = pl.multiple_of(first_ref[tile] * slot_len, slot_len)
    pick = pick_ref[pl.ds(here, TILE), :]
    bias = bias_ref[pl.ds(here, TILE), :]
    live = jnp.max(bias, axis=1, keepdims=True) > -1.0
    keys = k_pad[pl.ds(here, span), :]
    values = v_pad[pl.ds(here, span), :]
    scale = (HEAD_DIM**-0.5) * LOG2E
    for h in range(heads):
        cols = slice(h * HEAD_DIM, (h + 1) * HEAD_DIM)
        q = jnp.dot(
            pick, q_buf[pl.ds(begin, window), cols], preferred_element_type=jnp.float32
        ).astype(jnp.bfloat16)
        score = lax.dot_general(
            q, keys, (((1,), (1,)), ((), ())), preferred_element_type=jnp.float32
        )
        score = score * scale + bias
        peak = jnp.max(score, axis=1, keepdims=True)
        weight = jnp.exp2(score - peak)
        norm = jnp.sum(weight, axis=1, keepdims=True)
        mixed = jnp.dot(weight.astype(jnp.bfloat16), values, preferred_element_type=jnp.float32)
        out_ref[:, cols] = jnp.where(live, mixed / norm, 0.0).astype(jnp.bfloat16)


def attend(slot, first, q, kv, pick, bias, out, chunk, heads, kv_head, row_len, width):
    sentences, slot_len = slot.shape[0], q.shape[1]
    kv_width = kv.shape[2] // 2
    span = DOC_MAX + TILE
    chunk_width = heads * HEAD_DIM
    whole = pl.BlockSpec(memory_space=pltpu.VMEM)
    anywhere = pl.BlockSpec(memory_space=pl.ANY)
    operands = [slot, first, q, kv, pick, bias]
    specs = [anywhere, anywhere, whole, whole]
    aliases = {}
    if out is not None:
        operands.append(out)
        specs.append(anywhere)
        aliases = {6: 0}
    return pl.pallas_call(
        functools.partial(
            attend_kernel, kv_head=kv_head, kv_width=kv_width, heads=heads, span=span
        ),
        grid_spec=pltpu.PrefetchScalarGridSpec(
            num_scalar_prefetch=2,
            grid=(row_len // TILE,),
            in_specs=specs,
            out_specs=pl.BlockSpec((TILE, chunk_width), lambda t, *_: (t, chunk)),
            scratch_shapes=[
                pltpu.VMEM((sentences * slot_len, chunk_width), jnp.bfloat16),
                pltpu.VMEM((sentences * slot_len, 2 * kv_width), jnp.bfloat16),
                pltpu.VMEM((DOC_MAX + row_len, HEAD_DIM), jnp.bfloat16),
                pltpu.VMEM((DOC_MAX + row_len, HEAD_DIM), jnp.bfloat16),
                pltpu.SemaphoreType.DMA,
                pltpu.SemaphoreType.DMA,
            ],
        ),
        out_shape=jax.ShapeDtypeStruct((row_len, width), jnp.bfloat16),
        input_output_aliases=aliases,
        compiler_params=pltpu.CompilerParams(vmem_limit_bytes=32 << 20),
        cost_estimate=pl.CostEstimate(
            flops=4 * row_len * span * chunk_width,
            transcendentals=row_len * span * heads,
            bytes_accessed=6 * row_len * chunk_width,
        ),
        name="attend",
    )(*operands)


def per_device(queries, key_rows, value_rows, destination, token_count, doc_ids):
    groups = lax.axis_size("dp")
    ways = lax.axis_size("tensor")
    own_group = lax.axis_index("dp")
    sentences = destination.shape[0]
    slot_len = queries.shape[1]
    capacity = max(2, (2 * sentences + groups - 1) // groups)
    slots = groups * capacity
    row_len = doc_ids.shape[1]
    q_width = queries.shape[2]
    kv_width = key_rows.shape[2] // ways
    per_group = q_width // kv_width
    heads = min(CHUNK_HEADS, per_group)
    chunk_width = heads * HEAD_DIM

    def split(rows):
        return rows.reshape(rows.shape[0], slot_len, ways, kv_width)

    kv = jnp.concatenate([split(key_rows), split(value_rows)], axis=3)
    kv = lax.all_to_all(
        jnp.transpose(kv, (2, 0, 1, 3)), "tensor", split_axis=0, concat_axis=0, tiled=True
    ).reshape(sentences, slot_len, 2 * kv_width)

    order = jnp.arange(sentences, dtype=jnp.int32)
    same_dest = destination[:, None] == destination[None, :]
    earlier = order[None, :] < order[:, None]
    rank_in = jnp.sum((same_dest & earlier).astype(jnp.int32), axis=1)
    target = destination * capacity + rank_in

    def exchange(rows, col, width):
        return lax.all_to_all(
            bucket(rows, target, slots, col, width), "dp", split_axis=0, concat_axis=0, tiled=True
        )

    both = jnp.stack([destination, token_count])
    table = lax.all_gather(both, "dp", axis=0)
    mine = table[:, 0, :] == own_group
    place_rank = jnp.cumsum(mine.astype(jnp.int32), axis=1) - 1
    slot_ids = jnp.arange(capacity, dtype=jnp.int32)
    hits = mine[:, :, None] & (place_rank[:, :, None] == slot_ids[None, None, :])
    sizes = jnp.sum(jnp.where(hits, table[:, 1, :, None], 0), axis=1).reshape(slots)
    filled = sizes > 0
    nth = jnp.cumsum(filled.astype(jnp.int32)) - 1
    is_nth = filled[None, :] & (nth[None, :] == order[:, None])
    slot_of = jnp.sum(jnp.where(is_nth, jnp.arange(slots, dtype=jnp.int32)[None, :], 0), axis=1)
    count_of = jnp.sum(jnp.where(is_nth, sizes[None, :], 0), axis=1)
    ends = jnp.cumsum(count_of)
    total = ends[-1]
    place = jnp.arange(row_len, dtype=jnp.int32)
    passed = place[:, None] >= ends[None, :]
    which = jnp.sum(passed.astype(jnp.int32), axis=1)
    start = jnp.sum(jnp.where(passed, count_of[None, :], 0), axis=1)
    live = place < total
    flat = jnp.where(live, which * slot_len + place - start, -1)
    spread = min(sentences, (TILE - 1 + LEAST - 1) // LEAST + 1)
    first = jnp.minimum(which.reshape(-1, TILE)[:, 0], sentences - spread)
    window = spread * slot_len
    relative = flat - jnp.repeat(first, TILE) * slot_len
    pick = (
        live[:, None] & (relative[:, None] == jnp.arange(window, dtype=jnp.int32)[None, :])
    ).astype(jnp.bfloat16)
    span = DOC_MAX + TILE
    padded = jnp.concatenate([jnp.full((DOC_MAX,), -1, jnp.int32), doc_ids[0]])
    tiles = row_len // TILE
    key_docs = jnp.stack([padded[t * TILE : t * TILE + span] for t in range(tiles)])
    col = jnp.arange(span, dtype=jnp.int32)[None, None, :]
    row = jnp.arange(TILE, dtype=jnp.int32)[None, :, None]
    allowed = (
        (col - DOC_MAX <= row)
        & (key_docs[:, None, :] == doc_ids[0].reshape(tiles, TILE)[:, :, None])
        & live.reshape(tiles, TILE)[:, :, None]
    )
    bias = jnp.where(allowed, 0.0, NEG).astype(jnp.float32).reshape(row_len, span)

    got_kv = exchange(kv, 0, 2 * kv_width)
    out = None
    for chunk in range(q_width // chunk_width):
        got_q = exchange(queries, chunk * chunk_width, chunk_width)
        kv_head = chunk * heads // per_group
        out = attend(
            slot_of, first, got_q, got_kv, pick, bias, out, chunk, heads, kv_head, row_len, q_width
        )
    return out


def solution(mesh):
    placed = (
        P("dp", None, "tensor"),
        P(("dp", "tensor"), None, None),
        P(("dp", "tensor"), None, None),
        P("dp"),
        P("dp"),
        P("dp", None),
    )
    return jax.shard_map(
        per_device, mesh=mesh, in_specs=placed, out_specs=P("dp", "tensor"), check_vma=False
    )
```

time: 564 us -> 490 us (0.87)
  Pallas kernels: 0 us -> 416 us
  blocking collectives: 184 us -> 9.28 us
  matrix products: 97.6 us -> 0 us
  local copies, waits for them, and re-layouts: 79.1 us -> 4.55 us
  waiting for transfers between devices: 99.4 us -> 25 us
  other arithmetic: 75.2 us -> 5.75 us
  starting transfers between devices: 13 us -> 28.5 us
  between operations: 14.4 us -> 0.33 us
    pallas_call x0 -> x9, Pallas kernels: none -> 416 us  [the longest x5 295 us: bucket(): pl.pallas_call(functools.partial(bucket_kernel, col=col, width=width), gr...]
    unnamed x1 -> x0, blocking collectives: 184 us -> none
    dot_general x6 -> x0, matrix products: 97.6 us -> none  [the longest x3 51.6 us: per_device(): jnp.einsum('kgqs,skd->kgqd', weight.astype(jnp.bfloat16), v_tile, preferr...]
    all_gather x2 -> x0, waiting for transfers between devices: 92.4 us -> none  [the longest x1 47.8 us: per_device(): lax.all_gather(value_rows, 'tensor', axis=0, tiled=True)]
    gather x6 -> x0, local copies, waits for them, and re-layouts: 42.9 us -> none  [the longest x1 23 us: per_device(): packed_q = jnp.take(got_q.reshape(-1, got_q.shape[2]), flat_index, axis=0)]
    reduce_sum x6 -> x3, other arithmetic: 39.4 us -> 0.43 us  [the longest x1 0.21 us: per_device(): jnp.sum(jnp.where(hits, table[:, 1, :, None], 0), axis=1).reshape(slots)]
    select_n x9 -> x1, other arithmetic: 23.8 us -> 0.38 us  [per_device(): jnp.where(allowed, 0.0, NEG).astype(jnp.float32).reshape(row_len, span)]
    all_to_all x3 -> x6, waiting for transfers between devices: 5.63 us -> 25 us  [the longest x1 25 us: per_device(): lax.all_to_all(jnp.transpose(kv, (2, 0, 1, 3)), 'tensor', split_axis=0, c...]
  transfers between devices with their start and end apart: 5 -> 6, of which waited for: 4 -> 1; matrix products, arithmetic and copies ran while one was open for 7% -> 1% of each run, Pallas kernels for 0% -> 72%
where the time goes in v1:
time: 490 us; the launch traced here: 489 us
  Pallas kernels  416 us (85%)
  starting transfers between devices  28.5 us (6%)
  waiting for transfers between devices  25 us (5%)
  blocking collectives  9.28 us (2%)
  other arithmetic  5.75 us (1%)
    pallas_call x5, Pallas kernels, bucket(): pl.pallas_call(functools.partial(bucket_kernel, col=col, width=width), gr...  295 us
    pallas_call x4, Pallas kernels, attend(): pl.pallas_call(functools.partial(attend_kernel, kv_head=kv_head, kv_width...  121 us
    all_to_all x1, waiting for transfers between devices, per_device(): lax.all_to_all(jnp.transpose(kv, (2, 0, 1, 3)), 'tensor', split_axis=0, c...  25 us
    all_to_all x5, starting transfers between devices, exchange(): lax.all_to_all(bucket(rows, target, slots, col, width), 'dp', split_axis=...  22.2 us
  transfers between devices with their start and end apart: 6, of which 1 were waited for; matrix products, arithmetic and copies ran while one was open for 1% of the time, Pallas kernels for 72%

profile of v1, /device:TPU:0, one launch (start us, length us, event | category | flops | bytes accessed | tf_op | source)
XLA Modules:
  0.0 489.2 jit_solution(3367970256974709244)
XLA Ops:
  0.0 1.3 copy_bitcast_fusion
  1.3 1.1 maximum_bitcast_fusion
  2.4 6.3 %all-to-all-start.1 = ((bf16[4,8,32,512]{3,2,1,0:T(8,128)(2,1)}), bf16[4,8,32,512]{3,2,1,0:T(8,128)(2,1)S(1)}, u32[]{:S(2)}, u32[]{:S(2)}) async-start(bf16[4,8,32,512]{3,2,1,0:T(8,128)(2,1)} %maximum_bitcast_fusion), calls=%async_computation.1 | async-start | bytes 2097152 | tf_op jit(solution)/shard_map/all_to_all | solution.py:167
  8.7 0.2 convert_reduce_fusion.1
  8.9 0.6 multiply_add_fusion.target_ref
  9.5 25.0 %all-to-all-done.1 = bf16[4,8,32,512]{3,2,1,0:T(8,128)(2,1)S(1)} async-done(((bf16[4,8,32,512]{3,2,1,0:T(8,128)(2,1)}), bf16[4,8,32,512]{3,2,1,0:T(8,128)(2,1)S(1)}, u32[]{:S(2)}, u32[]{:S(2)}) %all-to-all-start.1) | async-done | bytes 1048608 | tf_op jit(solution)/shard_map/all_to_all | solution.py:167
  34.5 1.0 copy-done.2
  35.4 33.5 %bucket.6 = bf16[64,32,512]{2,1,0:T(8,128)(2,1)} custom-call(s32[32]{0:T(128)} %multiply_add_fusion.target_ref, bf16[32,32,512]{2,1,0:T(8,128)(2,1)} %bitcast.36), custom_call_target="tpu_custom_call" | custom-call | bytes 2097152 | tf_op jit(solution)/shard_map/bucket/pallas_call | solution.py:31
  69.0 3.7 all-to-all-start.2
  72.7 65.3 %bucket.9 = bf16[64,32,1024]{2,1,0:T(8,128)(2,1)} custom-call(s32[32]{0:T(128)} %multiply_add_fusion.target_ref, bf16[32,32,4096]{2,1,0:T(8,128)(2,1)} %rows_ref.7), custom_call_target="tpu_custom_call" | custom-call | bytes 4194304 | tf_op jit(solution)/shard_map/bucket/pallas_call | solution.py:31
  138.0 4.6 all-to-all-start.5
  142.6 65.3 %bucket.8 = bf16[64,32,1024]{2,1,0:T(8,128)(2,1)} custom-call(s32[32]{0:T(128)} %multiply_add_fusion.target_ref, bf16[32,32,4096]{2,1,0:T(8,128)(2,1)} %rows_ref.7), custom_call_target="tpu_custom_call" | custom-call | bytes 4194304 | tf_op jit(solution)/shard_map/bucket/pallas_call | solution.py:31
  207.9 4.6 all-to-all-start.4
  212.5 65.3 %bucket.7 = bf16[64,32,1024]{2,1,0:T(8,128)(2,1)} custom-call(s32[32]{0:T(128)} %multiply_add_fusion.target_ref, bf16[32,32,4096]{2,1,0:T(8,128)(2,1)} %rows_ref.7), custom_call_target="tpu_custom_call" | custom-call | bytes 4194304 | tf_op jit(solution)/shard_map/bucket/pallas_call | solution.py:31
  277.8 4.6 all-to-all-start.3
  282.4 65.4 %bucket.5 = bf16[64,32,1024]{2,1,0:T(8,128)(2,1)} custom-call(s32[32]{0:T(128)} %multiply_add_fusion.target_ref, bf16[32,32,4096]{2,1,0:T(8,128)(2,1)} %rows_ref.7), custom_call_target="tpu_custom_call" | custom-call | bytes 4194304 | tf_op jit(solution)/shard_map/bucket/pallas_call | solution.py:31
  347.9 9.3 %all-gather.1 = s32[8,2,32]{2,1,0:T(2,128)S(1)} all-gather(s32[1,2,32]{2,1,0:T(2,128)S(1)} %add_bitcast_fusion), channel_id=2, replica_groups=mesh['dp'=8,'tensor'=4] {'dp'}, dimensions={0}, use_global_device_ids=true | all-gather | bytes 2304 | tf_op jit(solution)/shard_map/all_gather | solution.py:183
  357.2 4.7 all-to-all-start
  362.0 0.2 reduce_window_sum.25
  362.1 0.2 select_reduce_fusion.1
  362.8 0.1 select_reduce_fusion.2
  363.0 0.5 slice.57
  363.7 0.7 fusion.8
  364.5 0.4 fusion.4.bias_ref
  364.9 0.7 iota_compare_fusion.6
  365.8 0.7 bitcast_subtract_fusion
  366.5 0.3 fusion.1.pick_ref
  366.8 30.2 %attend.4.rest_0_ = bf16[1024,4096]{1,0:T(8,128)(2,1)} custom-call(s32[32]{0:T(128)S(1)} %get-tuple-element.6.slot_ref, s32[8]{0:T(128)S(1)} %minimum_reduce_fusion.first_ref, bf16[64,32,1024]{2,1,0:T(8,128)(2,1)} %all-to-all-done.5.q_ref, bf16[64,32,512]{2,1,0:T(8,128)(2,1)S(1)} %all-to-all-done.2.kv_ref, bf16[1024,288]{1,0:T(8,128)(2,1)S(1)} %fusion.1.pick_ref, ...), custom_call_target="tpu_custom_call" | custom-call | flops 1610612736 | bytes 6291456 | tf_op jit(solution)/shard_map/attend/pallas_call | solution.py:118
  397.1 30.2 %attend.5.rest_0_ = bf16[1024,4096]{1,0:T(8,128)(2,1)} custom-call(s32[32]{0:T(128)S(1)} %get-tuple-element.6.slot_ref, s32[8]{0:T(128)S(1)} %minimum_reduce_fusion.first_ref, bf16[64,32,1024]{2,1,0:T(8,128)(2,1)} %all-to-all-done.4.q_ref, bf16[64,32,512]{2,1,0:T(8,128)(2,1)S(1)} %all-to-all-done.2.kv_ref, ...), custom_call_target="tpu_custom_call", output_to_operand_aliasing={{}: (6, {})} | custom-call | flops 1610612736 | bytes 6291456 | tf_op jit(solution)/shard_map/attend/pallas_call | solution.py:118
  427.3 30.2 %attend.6.rest_0_ = bf16[1024,4096]{1,0:T(8,128)(2,1)} custom-call(s32[32]{0:T(128)S(1)} %get-tuple-element.6.slot_ref, s32[8]{0:T(128)S(1)} %minimum_reduce_fusion.first_ref, bf16[64,32,1024]{2,1,0:T(8,128)(2,1)} %all-to-all-done.3.q_ref, bf16[64,32,512]{2,1,0:T(8,128)(2,1)S(1)} %all-to-all-done.2.kv_ref, ...), custom_call_target="tpu_custom_call", output_to_operand_aliasing={{}: (6, {})} | custom-call | flops 1610612736 | bytes 6291456 | tf_op jit(solution)/shard_map/attend/pallas_call | solution.py:118
  457.6 1.4 copy-done.1
  459.0 30.2 %attend.7 = bf16[1024,4096]{1,0:T(8,128)(2,1)} custom-call(s32[32]{0:T(128)S(1)} %get-tuple-element.6.slot_ref, s32[8]{0:T(128)S(1)} %minimum_reduce_fusion.first_ref, bf16[64,32,1024]{2,1,0:T(8,128)(2,1)} %all-to-all-done.q_ref, bf16[64,32,512]{2,1,0:T(8,128)(2,1)S(1)} %all-to-all-done.2.kv_ref, ...), custom_call_target="tpu_custom_call", output_to_operand_aliasing={{}: (6, {})} | custom-call | flops 1610612736 | bytes 6291456 | tf_op jit(solution)/shard_map/attend/pallas_call | solution.py:118
  (38 shorter events, 1.0 us)
Async XLA Ops:
  0.0 8.7 %copy-start.5 = (s32[32]{0:T(128)S(1)}, s32[32]{0:T(128)}, u32[]{:S(2)}) copy-start(s32[32]{0:T(128)} %param.9) | copy-start | bytes 388
  2.4 32.0 %all-to-all-start.1 = ((bf16[4,8,32,512]{3,2,1,0:T(8,128)(2,1)}), bf16[4,8,32,512]{3,2,1,0:T(8,128)(2,1)S(1)}, u32[]{:S(2)}, u32[]{:S(2)}) async-start(bf16[4,8,32,512]{3,2,1,0:T(8,128)(2,1)} %maximum_bitcast_fusion), calls=%async_computation.1 | async-start | bytes 2097152 | tf_op jit(solution)/shard_map/all_to_all | solution.py:167
  34.5 1.0 copy-start.2
  69.0 69.0 %all-to-all-start.2 = ((bf16[64,32,512]{2,1,0:T(8,128)(2,1)}), bf16[64,32,512]{2,1,0:T(8,128)(2,1)S(1)}, u32[]{:S(2)}, u32[]{:S(2)}) async-start(bf16[64,32,512]{2,1,0:T(8,128)(2,1)} %bucket.6), calls=%async_computation.2 | async-start | bytes 4194304 | tf_op jit(solution)/shard_map/all_to_all | solution.py:178
  138.0 69.9 %all-to-all-start.5 = ((bf16[64,32,1024]{2,1,0:T(8,128)(2,1)}), bf16[64,32,1024]{2,1,0:T(8,128)(2,1)}, u32[]{:S(2)}, u32[]{:S(2)}) async-start(bf16[64,32,1024]{2,1,0:T(8,128)(2,1)} %bucket.9), calls=%async_computation.5 | async-start | bytes 8388608 | tf_op jit(solution)/shard_map/all_to_all | solution.py:178
  207.9 69.9 %all-to-all-start.4 = ((bf16[64,32,1024]{2,1,0:T(8,128)(2,1)}), bf16[64,32,1024]{2,1,0:T(8,128)(2,1)}, u32[]{:S(2)}, u32[]{:S(2)}) async-start(bf16[64,32,1024]{2,1,0:T(8,128)(2,1)} %bucket.8), calls=%async_computation.4 | async-start | bytes 8388608 | tf_op jit(solution)/shard_map/all_to_all | solution.py:178
  277.8 79.4 %all-to-all-start.3 = ((bf16[64,32,1024]{2,1,0:T(8,128)(2,1)}), bf16[64,32,1024]{2,1,0:T(8,128)(2,1)}, u32[]{:S(2)}, u32[]{:S(2)}) async-start(bf16[64,32,1024]{2,1,0:T(8,128)(2,1)} %bucket.7), calls=%async_computation.3 | async-start | bytes 8388608 | tf_op jit(solution)/shard_map/all_to_all | solution.py:178
  282.4 65.5 %copy-start.4 = (s32[32]{0:T(128)S(1)}, s32[32]{0:T(128)}, u32[]{:S(2)}) copy-start(s32[32]{0:T(128)} %param.10) | copy-start | bytes 388
  357.2 6.5 %copy-start.3 = (s32[1,1024]{1,0:T(1,128)S(1)}, s32[1,1024]{1,0:T(1,128)}, u32[]{:S(2)}) copy-start(s32[1,1024]{1,0:T(1,128)} %param.11) | copy-start | bytes 12292
  357.2 100.4 %all-to-all-start = ((bf16[64,32,1024]{2,1,0:T(8,128)(2,1)}), bf16[64,32,1024]{2,1,0:T(8,128)(2,1)}, u32[]{:S(2)}, u32[]{:S(2)}) async-start(bf16[64,32,1024]{2,1,0:T(8,128)(2,1)} %bucket.5), calls=%async_computation | async-start | bytes 8388608 | tf_op jit(solution)/shard_map/all_to_all | solution.py:178
  364.8 62.5 %copy-start = (f32[1024,384]{1,0:T(8,128)}, f32[1024,384]{1,0:T(8,128)S(1)}, u32[]{:S(2)}) copy-start(f32[1024,384]{1,0:T(8,128)S(1)} %fusion.4.bias_ref) | copy-start | bytes 4718596
  457.6 1.4 copy-start.1

commit v2 on v1

v2 whole, which is shorter than its diff:
```python
import functools
import jax
import jax.numpy as jnp
from jax import lax
from jax.experimental import pallas as pl
from jax.experimental.pallas import tpu as pltpu
from jax.sharding import PartitionSpec as P

HEAD_DIM = 128
DOC_MAX = 256
LEAST = 16
TILE = 128
CHUNK_HEADS = 8
STACK = 4
NEG = -1e30
LOG2E = 1.4426950408889634
WHOLE = pl.BlockSpec(memory_space=pltpu.VMEM)
ANYWHERE = pl.BlockSpec(memory_space=pl.ANY)


def fetch(code_ref, sources, cols, bases, buf, sem):
    def one(k, carry):
        code = code_ref[k]
        for i, (source, col) in enumerate(zip(sources, cols)):

            def start(i=i, source=source, col=col):
                pltpu.make_async_copy(
                    source.at[code - bases[i], :, pl.ds(col, buf.shape[2])], buf.at[k], sem
                ).start()

            if len(sources) == 1:
                start()
            else:
                inside = code >= bases[i]
                if i + 1 < len(sources):
                    inside = inside & (code < bases[i + 1])
                pl.when(inside)(start)
        return carry

    lax.fori_loop(0, buf.shape[0], one, 0, unroll=4 if buf.shape[0] % 4 == 0 else 1)


def gather_kernel(code_ref, *rest, cols, bases):
    *sources, out_ref, sem = rest
    fetch(code_ref, sources, cols, bases, out_ref, sem)
    pltpu.make_async_copy(out_ref, out_ref, sem).wait()


def gather(codes, sources, cols, bases, width):
    slot_len = sources[0].shape[1]
    shape = (codes.shape[0], slot_len, width)
    return pl.pallas_call(
        functools.partial(gather_kernel, cols=cols, bases=bases),
        grid_spec=pltpu.PrefetchScalarGridSpec(
            num_scalar_prefetch=1,
            grid=(1,),
            in_specs=[ANYWHERE] * len(sources),
            out_specs=pl.BlockSpec(shape, lambda i, *_: (0, 0, 0)),
            scratch_shapes=[pltpu.SemaphoreType.DMA],
        ),
        out_shape=jax.ShapeDtypeStruct(shape, sources[0].dtype),
        compiler_params=pltpu.CompilerParams(vmem_limit_bytes=16 << 20),
        cost_estimate=pl.CostEstimate(
            flops=0, transcendentals=0, bytes_accessed=4 * shape[0] * slot_len * width
        ),
        name="gather",
    )(codes, *sources)


def pack_kernel(code_ref, first_ref, pick_ref, *rest, cols, bases):
    *sources, k_ref, v_ref, buf, sem = rest
    kv_local, slot_len, window = k_ref.shape[0], buf.shape[1], pick_ref.shape[1]
    fetch(code_ref, sources, cols, bases, buf, sem)
    pltpu.make_async_copy(buf, buf, sem).wait()
    for ref in (k_ref, v_ref):
        ref[:, :DOC_MAX, :] = jnp.zeros((kv_local, DOC_MAX, HEAD_DIM), jnp.bfloat16)

    @pl.loop(0, pick_ref.shape[0] // TILE)
    def _(t):
        here = pl.multiple_of(t * TILE, TILE)
        rows = buf[pl.ds(first_ref[t], window // slot_len)].reshape(window, buf.shape[2])
        packed = jnp.dot(
            pick_ref[pl.ds(here, TILE), :], rows, preferred_element_type=jnp.float32
        ).astype(jnp.bfloat16)
        for n in range(2 * kv_local):
            ref = (k_ref, v_ref)[n // kv_local]
            ref[n % kv_local, pl.ds(DOC_MAX + here, TILE), :] = packed[
                :, n * HEAD_DIM : (n + 1) * HEAD_DIM
            ]


def pack(codes, first, pick, sources, cols, bases, kv_local):
    slot_len = sources[0].shape[1]
    shape = jax.ShapeDtypeStruct((kv_local, DOC_MAX + pick.shape[0], HEAD_DIM), jnp.bfloat16)
    return pl.pallas_call(
        functools.partial(pack_kernel, cols=cols, bases=bases),
        grid_spec=pltpu.PrefetchScalarGridSpec(
            num_scalar_prefetch=2,
            grid=(1,),
            in_specs=[WHOLE] + [ANYWHERE] * len(sources),
            out_specs=[WHOLE, WHOLE],
            scratch_shapes=[
                pltpu.VMEM((codes.shape[0], slot_len, 2 * kv_local * HEAD_DIM), jnp.bfloat16),
                pltpu.SemaphoreType.DMA,
            ],
        ),
        out_shape=[shape, shape],
        compiler_params=pltpu.CompilerParams(vmem_limit_bytes=16 << 20),
        name="pack",
    )(codes, first, pick, *sources)


def attend_kernel(code_ref, first_ref, k_ref, v_ref, pick_ref, bias_ref, *rest, cols, bases, heads):
    *sources, out_ref, q_buf, q_rows, sem = rest
    sources = sources[: len(cols)]
    tile = pl.program_id(0)
    slot_len, window = q_buf.shape[1], pick_ref.shape[1]
    span = bias_ref.shape[1]

    @pl.when(tile == 0)
    def _():
        fetch(code_ref, sources, cols, bases, q_buf, sem)
        pltpu.make_async_copy(q_buf, q_buf, sem).wait()

    here = pl.multiple_of(tile * TILE, TILE)
    pick = pick_ref[pl.ds(here, TILE), :]
    bias = bias_ref[pl.ds(here, TILE), :]
    live = jnp.max(bias, axis=1, keepdims=True) > -1.0
    keys = k_ref[pl.ds(here, span), :]
    values = v_ref[pl.ds(here, span), :]
    rows = q_buf[pl.ds(first_ref[tile], window // slot_len)].reshape(window, q_buf.shape[2])
    packed = jnp.dot(pick, rows, preferred_element_type=jnp.float32).astype(jnp.bfloat16)
    for h in range(heads):
        q_rows[h * TILE : (h + 1) * TILE, :] = packed[:, h * HEAD_DIM : (h + 1) * HEAD_DIM]
    scale = (HEAD_DIM**-0.5) * LOG2E
    stack = min(STACK, heads)
    for g in range(heads // stack):
        score = lax.dot_general(
            q_rows[g * stack * TILE : (g + 1) * stack * TILE, :],
            keys,
            (((1,), (1,)), ((), ())),
            preferred_element_type=jnp.float32,
        ).reshape(stack, TILE, span)
        score = score * scale + bias[None]
        peak = jnp.max(score, axis=2, keepdims=True)
        weight = jnp.exp2(score - peak)
        norm = jnp.sum(weight, axis=2, keepdims=True)
        mixed = jnp.dot(
            weight.astype(jnp.bfloat16).reshape(stack * TILE, span),
            values,
            preferred_element_type=jnp.float32,
        ).reshape(stack, TILE, HEAD_DIM)
        result = jnp.where(live[None], mixed / norm, 0.0).astype(jnp.bfloat16)
        for n in range(stack):
            h = g * stack + n
            out_ref[:, h * HEAD_DIM : (h + 1) * HEAD_DIM] = result[n]


def attend(codes, first, keys, values, pick, bias, sources, cols, bases, out, chunk, heads, kv_head, width):
    slot_len, (row_len, span) = sources[0].shape[1], bias.shape
    chunk_width = heads * HEAD_DIM
    one_head = pl.BlockSpec((None, DOC_MAX + row_len, HEAD_DIM), lambda t, *_: (kv_head, 0, 0))
    operands = [codes, first, keys, values, pick, bias, *sources]
    specs = [one_head, one_head, WHOLE, WHOLE] + [ANYWHERE] * len(sources)
    aliases = {}
    if out is not None:
        aliases = {len(operands): 0}
        operands.append(out)
        specs.append(ANYWHERE)
    return pl.pallas_call(
        functools.partial(attend_kernel, cols=cols, bases=bases, heads=heads),
        grid_spec=pltpu.PrefetchScalarGridSpec(
            num_scalar_prefetch=2,
            grid=(row_len // TILE,),
            in_specs=specs,
            out_specs=pl.BlockSpec((TILE, chunk_width), lambda t, *_: (t, chunk)),
            scratch_shapes=[
                pltpu.VMEM((codes.shape[0], slot_len, chunk_width), jnp.bfloat16),
                pltpu.VMEM((heads * TILE, HEAD_DIM), jnp.bfloat16),
                pltpu.SemaphoreType.DMA,
            ],
        ),
        out_shape=jax.ShapeDtypeStruct((row_len, width), jnp.bfloat16),
        input_output_aliases=aliases,
        compiler_params=pltpu.CompilerParams(vmem_limit_bytes=32 << 20),
        cost_estimate=pl.CostEstimate(
            flops=4 * row_len * span * chunk_width,
            transcendentals=row_len * span * heads,
            bytes_accessed=6 * row_len * chunk_width,
        ),
        name="attend",
    )(*operands)


def flip(rows, bit):
    pairs = [(i, i ^ bit) for i in range(lax.axis_size("dp"))]
    return lax.ppermute(rows, "dp", pairs)


def lists_of(masks, codes, slots):
    items = masks.shape[1]
    upto = jnp.arange(items)[:, None] <= jnp.arange(items)[None, :]
    rank = jnp.dot(
        masks.astype(jnp.bfloat16), upto.astype(jnp.bfloat16), preferred_element_type=jnp.float32
    ).astype(jnp.int32) - 1
    rank = jnp.where(masks, rank, -1)
    if codes is None:
        return rank
    at = rank[:, None, :] == jnp.arange(slots, dtype=jnp.int32)[None, :, None]
    return jnp.sum(jnp.where(at, codes, 0), axis=2)


def hop_tables(dest, source, lane, me, groups, sentences, first_bit, second_bit):
    cross1 = ((dest ^ source) & first_bit) != 0
    place1 = jnp.where(cross1, source ^ first_bit, source)
    cross2 = ((dest ^ source) & second_bit) != 0
    place2 = jnp.where(cross2, place1 ^ second_bit, place1)
    cross3 = ((dest ^ source) & 1) != 0
    arrive = [
        (source == me ^ first_bit) & cross1,
        (place1 == me ^ second_bit) & cross2,
        (place2 == me ^ 1) & cross3,
    ]
    rank = lists_of(jnp.stack(arrive), None, None)
    away = source ^ me
    code = jnp.where(
        away == 0,
        lane,
        jnp.where(
            (away & 1) != 0,
            3 * sentences + rank[2],
            jnp.where((away & second_bit) != 0, 2 * sentences + rank[1], sentences + rank[0]),
        ),
    )
    send = [
        (source == me) & cross1,
        (place1 == me) & cross2,
        (place2 == me) & cross3,
        dest == me,
    ]
    lists = lists_of(jnp.stack(send), code[None, None, :], sentences)
    every = jnp.arange(groups, dtype=jnp.int32)[:, None]
    loads = [
        jnp.sum(((at[None, :] == every) & cross[None, :]).astype(jnp.int32), axis=1)
        for at, cross in ((source, cross1), (place1, cross2), (place2, cross3))
    ]
    return lists, jnp.max(jnp.stack(loads))


def journey(rows, col, width, lists, cap, bits, sentences):
    sources, cols = [rows], [col]
    bases = tuple(n * sentences for n in range(4))
    for hop, bit in enumerate((*bits, 1)):
        sent = gather(
            lists[hop, :cap], sources, tuple(cols), bases[: len(sources)], width
        )
        sources, cols = sources + [flip(sent, bit)], cols + [0]
    return sources, tuple(cols), bases


def per_device(queries, key_rows, value_rows, destination, token_count, doc_ids):
    groups = lax.axis_size("dp")
    ways = lax.axis_size("tensor")
    me = lax.axis_index("dp")
    sentences = destination.shape[0]
    slot_len = queries.shape[1]
    row_len = doc_ids.shape[1]
    q_width = queries.shape[2]
    kv_width = key_rows.shape[2] // ways
    kv_local = kv_width // HEAD_DIM
    per_group = q_width // kv_width
    heads = min(CHUNK_HEADS, per_group)
    chunk_width = heads * HEAD_DIM

    table = lax.all_gather(jnp.stack([destination, token_count]), "dp", axis=0)

    def split(rows):
        return rows.reshape(rows.shape[0], slot_len, ways, kv_width)

    kv = jnp.concatenate([split(key_rows), split(value_rows)], axis=3)
    kv = lax.all_to_all(
        jnp.transpose(kv, (2, 0, 1, 3)), "tensor", split_axis=0, concat_axis=0, tiled=True
    ).reshape(sentences, slot_len, 2 * kv_width)

    dest = table[:, 0, :].reshape(-1)
    counts = table[:, 1, :].reshape(-1)
    source = jnp.repeat(jnp.arange(groups, dtype=jnp.int32), sentences)
    lane = jnp.tile(jnp.arange(sentences, dtype=jnp.int32), groups)

    count_of = lists_of((dest == me)[None], counts[None, None, :], sentences)[0]
    nth = jnp.arange(sentences, dtype=jnp.int32)
    ends = jnp.sum(jnp.where(nth[None, :] <= nth[:, None], count_of[None, :], 0), axis=1)
    place = jnp.arange(row_len, dtype=jnp.int32)
    passed = place[:, None] >= ends[None, :]
    which = jnp.sum(passed.astype(jnp.int32), axis=1)
    start = jnp.sum(jnp.where(passed, count_of[None, :], 0), axis=1)
    live = which < sentences
    spread = min(sentences, (TILE - 1 + LEAST - 1) // LEAST + 1)
    heads_of = place[::TILE]
    first = jnp.sum((heads_of[:, None] >= ends[None, :]).astype(jnp.int32), axis=1)
    first = jnp.minimum(first, sentences - spread)
    window = spread * slot_len
    relative = (which - jnp.repeat(first, TILE)) * slot_len + place - start
    pick = (
        live[:, None] & (relative[:, None] == jnp.arange(window, dtype=jnp.int32)[None, :])
    ).astype(jnp.bfloat16)
    span = DOC_MAX + TILE
    padded = jnp.concatenate([jnp.full((DOC_MAX,), -1, jnp.int32), doc_ids[0]])
    tiles = row_len // TILE
    key_docs = jnp.stack([padded[t * TILE : t * TILE + span] for t in range(tiles)])
    col = jnp.arange(span, dtype=jnp.int32)[None, None, :]
    row = jnp.arange(TILE, dtype=jnp.int32)[None, :, None]
    allowed = (
        (col - DOC_MAX <= row)
        & (key_docs[:, None, :] == doc_ids[0].reshape(tiles, TILE)[:, :, None])
        & live.reshape(tiles, TILE)[:, :, None]
    )
    bias = jnp.where(allowed, 0.0, NEG).astype(jnp.float32).reshape(row_len, span)

    chunks = q_width // chunk_width

    def attend_all(got_kv, kv_codes, got_q, q_codes):
        keys, values = pack(kv_codes, first, pick, *got_kv, kv_local)
        out = None
        turn = sorted(range(chunks), key=lambda n: (n % (chunks // 2 or 1), n))
        for chunk in turn:
            kv_head = chunk * heads // per_group
            out = attend(
                q_codes[chunk], first, keys, values, pick, bias, *got_q[chunk], out, chunk, heads,
                kv_head, q_width,
            )
        return out

    if groups != 8:
        capacity = max(2, (2 * sentences + groups - 1) // groups)
        rank = lists_of(destination[None, :] == jnp.arange(groups, dtype=jnp.int32)[:, None], None, None)
        slot = jnp.arange(capacity, dtype=jnp.int32)
        at = rank[:, None, :] == slot[None, :, None]
        picked = jnp.sum(jnp.where(at, nth[None, None, :], 0), axis=2).reshape(-1)
        by_source = (dest == me).reshape(groups, sentences)
        rank_in = lists_of(by_source, None, None).reshape(-1)
        codes = lists_of(
            (dest == me)[None], (source * capacity + rank_in)[None, None, :], sentences
        )[0]

        def exchange(rows, col, width):
            sent = gather(picked, [rows], (col,), (0,), width)
            got = lax.all_to_all(sent, "dp", split_axis=0, concat_axis=0, tiled=True)
            return [got], (0,), (0,)

        got_kv = exchange(kv, 0, 2 * kv_width)
        got_q = [exchange(queries, n * chunk_width, chunk_width) for n in range(chunks)]
        return attend_all(got_kv, codes, got_q, [codes] * chunks)

    bits = ((2, 4), (4, 2))
    tables, loads = zip(
        *(hop_tables(dest, source, lane, me, groups, sentences, *pair) for pair in bits)
    )
    most = jnp.maximum(*loads)
    caps = sorted({min(sentences, n) for n in (20, 22, 25, sentences)})

    def with_cap(cap, queries, kv, *tables):
        got_q = []
        for n in range(chunks):
            half = n * 2 // chunks
            got_q.append(
                journey(queries, n * chunk_width, chunk_width, tables[half], cap, bits[half], sentences)
            )
        got_kv = journey(kv, 0, 2 * kv_width, tables[0], cap, bits[0], sentences)
        return attend_all(
            got_kv, tables[0][3], got_q, [tables[n * 2 // chunks][3] for n in range(chunks)]
        )

    tier = sum((most > cap).astype(jnp.int32) for cap in caps[:-1])
    return lax.switch(
        tier, [functools.partial(with_cap, cap) for cap in caps], queries, kv, *tables
    )


def solution(mesh):
    placed = (
        P("dp", None, "tensor"),
        P(("dp", "tensor"), None, None),
        P(("dp", "tensor"), None, None),
        P("dp"),
        P("dp"),
        P("dp", None),
    )
    return jax.shard_map(
        per_device, mesh=mesh, in_specs=placed, out_specs=P("dp", "tensor"), check_vma=False
    )
```

time: 490 us -> 338 us (0.69)
  Pallas kernels: 416 us -> 91.6 us
  waiting for transfers between devices: 25 us -> 191 us
  starting transfers between devices: 28.5 us -> 21.8 us
    pallas_call x9 -> x20, Pallas kernels: 416 us -> 91.6 us  [the longest x4 50.6 us: attend(): pl.pallas_call(functools.partial(attend_kernel, cols=cols, bases=bases, h...]
    ppermute x0 -> x15, waiting for transfers between devices: none -> 185 us  [flip(): return lax.ppermute(rows, 'dp', pairs)]
    all_to_all x5 -> x0, starting transfers between devices: 22.2 us -> none  [exchange(): lax.all_to_all(bucket(rows, target, slots, col, width), 'dp', split_axis=...]
    all_to_all x1, waiting for transfers between devices: 25 us -> 6.43 us  [per_device(): lax.all_to_all(jnp.transpose(kv, (2, 0, 1, 3)), 'tensor', split_axis=0, c...]
    ppermute x0 -> x15, starting transfers between devices: none -> 15.3 us  [flip(): return lax.ppermute(rows, 'dp', pairs)]
  transfers between devices with their start and end apart: 6 -> 16, of which waited for: 1 -> 6; matrix products, arithmetic and copies ran while one was open for 1% -> 2% of each run, Pallas kernels for 72% -> 23%
where the time goes in v2:
time: 338 us; the launch traced here: 334 us
  waiting for transfers between devices  191 us (57%)
  Pallas kernels  91.6 us (27%)
  starting transfers between devices  21.8 us (6%)
  blocking collectives  8.9 us (3%)
  local copies, waits for them, and re-layouts  7.71 us (2%)
  other arithmetic  6.47 us (2%)
  between operations  4.14 us (1%)
    ppermute x15, waiting for transfers between devices, flip(): return lax.ppermute(rows, 'dp', pairs)  185 us
    pallas_call x4, Pallas kernels, attend(): pl.pallas_call(functools.partial(attend_kernel, cols=cols, bases=bases, h...  50.6 us
    pallas_call x15, Pallas kernels, gather(): pl.pallas_call(functools.partial(gather_kernel, cols=cols, bases=bases),...  36.4 us
    ppermute x15, starting transfers between devices, flip(): return lax.ppermute(rows, 'dp', pairs)  15.3 us
    all_gather x1, blocking collectives, per_device(): table = lax.all_gather(jnp.stack([destination, token_count]), 'dp', axis=0)  8.9 us
  transfers between devices with their start and end apart: 16, of which 6 were waited for; matrix products, arithmetic and copies ran while one was open for 2% of the time, Pallas kernels for 23%

profile of v2, /device:TPU:0, one launch (start us, length us, event | category | flops | bytes accessed | tf_op | source)
XLA Modules:
  0.0 333.7 jit_solution(10100398390757029873)
XLA Ops:
  4.6 6.4 %all-to-all-start = ((bf16[4,8,32,512]{3,2,1,0:T(8,128)(2,1)}), bf16[4,8,32,512]{3,2,1,0:T(8,128)(2,1)S(1)}, u32[]{:S(2)}, u32[]{:S(2)}) async-start(bf16[4,8,32,512]{3,2,1,0:T(8,128)(2,1)} %copy.32), calls=%async_computation | async-start | bytes 2097152 | tf_op jit(solution)/shard_map/all_to_all | solution.py:281
  11.0 8.9 %all-gather.1 = s32[8,2,32]{2,1,0:T(2,128)S(1)} all-gather(s32[1,2,32]{2,1,0:T(2,128)S(1)} %add_bitcast_fusion), channel_id=2, replica_groups=mesh['dp'=8,'tensor'=4] {'dp'}, dimensions={0}, use_global_device_ids=true | all-gather | bytes 2304 | tf_op jit(solution)/shard_map/all_gather | solution.py:275
  30.3 6.4 %all-to-all-done = bf16[4,8,32,512]{3,2,1,0:T(8,128)(2,1)S(1)} async-done(((bf16[4,8,32,512]{3,2,1,0:T(8,128)(2,1)}), bf16[4,8,32,512]{3,2,1,0:T(8,128)(2,1)S(1)}, u32[]{:S(2)}, u32[]{:S(2)}) %all-to-all-start) | async-done | bytes 1048608 | tf_op jit(solution)/shard_map/all_to_all | solution.py:281
  36.9 296.7 %conditional.1 = (bf16[1024,4096]{1,0:T(8,128)(2,1)}) conditional(s32[]{:T(128)} %clamp.3, (pred[4,256]{1,0:T(4,128)(4,1)S(1)}, pred[4,256]{1,0:T(4,128)(4,1)S(1)}, bf16[4,8,32,512]{3,2,1,0:T(8,128)(2,1)S(1)}, s32[8]{0:T(128)S(1)}, bf16[1024,288]{1,0:T(8,128)(2,1)S(1)}, /*index=5*/bf16[32,32,4096]{2,1,0:T(8,128)(2,1)}, ...), branch_computations={%region_19.20_spmd, %region_20.21_spmd, %region_21.22_spmd, %regio... | conditional | flops 6444281856 | bytes 247604928 | solution.py:375
  37.7 2.6 gather.117
  43.4 1.7 collective-permute-start.54
  49.7 39.2 %collective-permute-done.57.rest_1_ = bf16[32,32,1024]{2,1,0:T(8,128)(2,1)S(1)} collective-permute-done((bf16[32,32,1024]{2,1,0:T(8,128)(2,1)S(1)}, bf16[32,32,1024]{2,1,0:T(8,128)(2,1)S(1)}, u32[]{:S(2)}, u32[]{:S(2)}) %collective-permute-start.57) | collective-permute-done | bytes 2097184 | tf_op jit(solution)/shard_map/cond/branch_3_fun/ppermute | solution.py:197
  88.9 1.9 gather.118
  90.8 2.1 collective-permute-start.58
  92.8 2.2 gather.115
  95.1 1.6 collective-permute-start.55
  96.7 37.1 %collective-permute-done.51.rest_1_ = bf16[32,32,1024]{2,1,0:T(8,128)(2,1)S(1)} collective-permute-done((bf16[32,32,1024]{2,1,0:T(8,128)(2,1)S(1)}, bf16[32,32,1024]{2,1,0:T(8,128)(2,1)S(1)}, u32[]{:S(2)}, u32[]{:S(2)}) %collective-permute-start.51) | collective-permute-done | bytes 2097184 | tf_op jit(solution)/shard_map/cond/branch_3_fun/ppermute | solution.py:197
  133.8 1.9 gather.112
  135.7 2.1 collective-permute-start.52
  137.8 2.2 gather.109
  140.0 1.6 collective-permute-start.49
  141.6 2.1 gather.105
  144.2 100.0 %collective-permute-done.45.rest_1_ = bf16[32,32,512]{2,1,0:T(8,128)(2,1)S(1)} collective-permute-done((bf16[32,32,512]{2,1,0:T(8,128)(2,1)S(1)}, bf16[32,32,512]{2,1,0:T(8,128)(2,1)S(1)}, u32[]{:S(2)}, u32[]{:S(2)}) %collective-permute-start.45) | collective-permute-done | bytes 1048608 | tf_op jit(solution)/shard_map/cond/branch_3_fun/ppermute | solution.py:197
  244.2 2.3 gather.106
  248.0 2.8 gather.119
  250.9 4.1 %gather.116 = bf16[32,32,1024]{2,1,0:T(8,128)(2,1)} custom-call(s32[32]{0:T(128)S(1)} %get-tuple-element.894.code_ref, bf16[32,32,4096]{2,1,0:T(8,128)(2,1)S(1)} %copy-done.5, bf16[32,32,1024]{2,1,0:T(8,128)(2,1)S(1)} %collective-permute-done.54.rest_1_, bf16[32,32,1024]{2,1,0:T(8,128)(2,1)S(1)} %collective-permute-done.55.rest_2_), custom_call_target="tpu_custom_call" | custom-call | bytes 4194304 | tf_op jit(solution)/shard_map/cond/branch_3_fun/gather/pallas_call | solution.py:52
  255.1 4.1 %gather.113 = bf16[32,32,1024]{2,1,0:T(8,128)(2,1)} custom-call(s32[32]{0:T(128)S(1)} %get-tuple-element.898.code_ref, bf16[32,32,4096]{2,1,0:T(8,128)(2,1)S(1)} %copy-done.5, bf16[32,32,1024]{2,1,0:T(8,128)(2,1)S(1)} %collective-permute-done.51.rest_1_, bf16[32,32,1024]{2,1,0:T(8,128)(2,1)S(1)} %collective-permute-done.52.rest_2_), custom_call_target="tpu_custom_call" | custom-call | bytes 4194304 | tf_op jit(solution)/shard_map/cond/branch_3_fun/gather/pallas_call | solution.py:52
  259.4 3.6 %gather.110 = bf16[32,32,1024]{2,1,0:T(8,128)(2,1)S(1)} custom-call(s32[32]{0:T(128)S(1)} %get-tuple-element.894.code_ref, bf16[32,32,4096]{2,1,0:T(8,128)(2,1)} %get-tuple-element.166.rest_0_, bf16[32,32,1024]{2,1,0:T(8,128)(2,1)S(1)} %collective-permute-done.48.rest_1_, bf16[32,32,1024]{2,1,0:T(8,128)(2,1)S(1)} %collective-permute-done.49.rest_2_), custom_call_target="tpu_custom_call" | custom-call | bytes 4194304 | tf_op jit(solution)/shard_map/cond/branch_3_fun/gather/pallas_call | solution.py:52
  263.6 6.3 %collective-permute-done.46.rest_2_ = bf16[32,32,512]{2,1,0:T(8,128)(2,1)S(1)} collective-permute-done((bf16[32,32,512]{2,1,0:T(8,128)(2,1)S(1)}, bf16[32,32,512]{2,1,0:T(8,128)(2,1)S(1)}, u32[]{:S(2)}, u32[]{:S(2)}) %collective-permute-start.46) | collective-permute-done | bytes 1048608 | tf_op jit(solution)/shard_map/cond/branch_3_fun/ppermute | solution.py:197
  269.8 2.5 gather.107
  272.8 2.2 collective-permute-done.47.rest_3_
  275.0 4.6 %pack.7 = (bf16[2,1280,128]{2,1,0:T(8,128)(2,1)S(1)}, bf16[2,1280,128]{2,1,0:T(8,128)(2,1)S(1)}) custom-call(s32[32]{0:T(128)S(1)} %get-tuple-element.901.code_ref, s32[8]{0:T(128)S(1)} %get-tuple-element.94.first_ref, bf16[1024,288]{1,0:T(8,128)(2,1)S(1)} %get-tuple-element.96.pick_ref, bf16[32,32,512]{2,1,0:T(8,128)(2,1)S(1)} %bitcast.169, ...), custom_call_target="tpu_custom_call" | custom-call | tf_op jit(solution)/shard_map/cond/branch_3_fun/pack/pallas_call | solution.py:95
  281.0 1.6 copy-done.1
  282.6 12.6 %attend.28.rest_4_ = bf16[1024,4096]{1,0:T(8,128)(2,1)} custom-call(s32[32]{0:T(128)S(1)} %get-tuple-element.901.code_ref, s32[8]{0:T(128)S(1)} %get-tuple-element.94.first_ref, bf16[2,1280,128]{2,1,0:T(8,128)(2,1)S(1)} %get-tuple-element.98.k_ref, bf16[2,1280,128]{2,1,0:T(8,128)(2,1)S(1)} %get-tuple-element.99.v_ref, ...), custom_call_target="tpu_custom_call" | custom-call | flops 1610612736 | bytes 6291456 | tf_op jit(solution)/shard_map/cond/branch_3_fun/attend/pallas_call | solution.py:170
  295.2 12.6 %attend.29.rest_4_ = bf16[1024,4096]{1,0:T(8,128)(2,1)} custom-call(s32[32]{0:T(128)S(1)} %get-tuple-element.897.code_ref, s32[8]{0:T(128)S(1)} %get-tuple-element.94.first_ref, bf16[2,1280,128]{2,1,0:T(8,128)(2,1)S(1)} %get-tuple-element.98.k_ref, bf16[2,1280,128]{2,1,0:T(8,128)(2,1)S(1)} %get-tuple-element.99.v_ref, ...), custom_call_target="tpu_custom_call", output_to_operand_aliasing={{}: (10, {})} | custom-call | flops 1610612736 | bytes 6291456 | tf_op jit(solution)/shard_map/cond/branch_3_fun/attend/pallas_call | solution.py:170
  307.9 12.6 %attend.30.rest_4_ = bf16[1024,4096]{1,0:T(8,128)(2,1)} custom-call(s32[32]{0:T(128)S(1)} %get-tuple-element.901.code_ref, s32[8]{0:T(128)S(1)} %get-tuple-element.94.first_ref, bf16[2,1280,128]{2,1,0:T(8,128)(2,1)S(1)} %get-tuple-element.98.k_ref, bf16[2,1280,128]{2,1,0:T(8,128)(2,1)S(1)} %get-tuple-element.99.v_ref, ...), custom_call_target="tpu_custom_call", output_to_operand_aliasing={{}: (10, {})} | custom-call | flops 1610612736 | bytes 6291456 | tf_op jit(solution)/shard_map/cond/branch_3_fun/attend/pallas_call | solution.py:170
  320.6 12.6 %attend.31 = bf16[1024,4096]{1,0:T(8,128)(2,1)} custom-call(s32[32]{0:T(128)S(1)} %get-tuple-element.897.code_ref, s32[8]{0:T(128)S(1)} %get-tuple-element.94.first_ref, bf16[2,1280,128]{2,1,0:T(8,128)(2,1)S(1)} %get-tuple-element.98.k_ref, bf16[2,1280,128]{2,1,0:T(8,128)(2,1)S(1)} %get-tuple-element.99.v_ref, ...), custom_call_target="tpu_custom_call", output_to_operand_aliasing={{}: (10, {})} | custom-call | flops 1610612736 | bytes 6291456 | tf_op jit(solution)/shard_map/cond/branch_3_fun/attend/pallas_call | solution.py:170
  (110 shorter events, 23.8 us)
Async XLA Ops:
  4.6 6.5 %copy-start.12 = (s32[32]{0:T(128)S(1)}, s32[32]{0:T(128)}, u32[]{:S(2)}) copy-start(s32[32]{0:T(128)} %param.14) | copy-start | bytes 388
  4.6 6.5 %copy-start.13 = (s32[32]{0:T(128)S(1)}, s32[32]{0:T(128)}, u32[]{:S(2)}) copy-start(s32[32]{0:T(128)} %param.13) | copy-start | bytes 388
  4.6 16.7 %copy-start.11 = (s32[1,1024]{1,0:T(1,128)S(1)}, s32[1,1024]{1,0:T(1,128)}, u32[]{:S(2)}) copy-start(s32[1,1024]{1,0:T(1,128)} %param.15) | copy-start | bytes 12292
  4.6 32.2 %all-to-all-start = ((bf16[4,8,32,512]{3,2,1,0:T(8,128)(2,1)}), bf16[4,8,32,512]{3,2,1,0:T(8,128)(2,1)S(1)}, u32[]{:S(2)}, u32[]{:S(2)}) async-start(bf16[4,8,32,512]{3,2,1,0:T(8,128)(2,1)} %copy.32), calls=%async_computation | async-start | bytes 2097152 | tf_op jit(solution)/shard_map/all_to_all | solution.py:281
  37.7 4.3 %copy-start.5 = (bf16[32,32,4096]{2,1,0:T(8,128)(2,1)S(1)}, bf16[32,32,4096]{2,1,0:T(8,128)(2,1)}, u32[]{:S(2)}) copy-start(bf16[32,32,4096]{2,1,0:T(8,128)(2,1)} %get-tuple-element.166.rest_0_) | copy-start | bytes 25165828 | tf_op jit(solution)/shard_map/cond
  40.2 48.6 %collective-permute-start.57 = (bf16[32,32,1024]{2,1,0:T(8,128)(2,1)S(1)}, bf16[32,32,1024]{2,1,0:T(8,128)(2,1)S(1)}, u32[]{:S(2)}, u32[]{:S(2)}) collective-permute-start(bf16[32,32,1024]{2,1,0:T(8,128)(2,1)S(1)} %gather.117), channel_id=1, source_target_pairs={{0,8},{4,12},{8,0},{12,4},{16,24},{20,28},{24,16},{28,20},{1,9},{5... | collective-permute-start | bytes 6291464 | tf_op jit(solution)/shard_map/cond/branch_3_fun/ppermute | solution.py:197
  43.4 49.5 %collective-permute-start.54 = (bf16[32,32,1024]{2,1,0:T(8,128)(2,1)S(1)}, bf16[32,32,1024]{2,1,0:T(8,128)(2,1)S(1)}, u32[]{:S(2)}, u32[]{:S(2)}) collective-permute-start(bf16[32,32,1024]{2,1,0:T(8,128)(2,1)S(1)} %gather.114), channel_id=1, source_target_pairs={{0,16},{4,20},{8,24},{12,28},{16,0},{20,4},{24,8},{28,12},{1,17},{... | collective-permute-start | bytes 6291464 | tf_op jit(solution)/shard_map/cond/branch_3_fun/ppermute | solution.py:197
  46.5 87.3 %collective-permute-start.51 = (bf16[32,32,1024]{2,1,0:T(8,128)(2,1)S(1)}, bf16[32,32,1024]{2,1,0:T(8,128)(2,1)S(1)}, u32[]{:S(2)}, u32[]{:S(2)}) collective-permute-start(bf16[32,32,1024]{2,1,0:T(8,128)(2,1)S(1)} %gather.111), channel_id=1, source_target_pairs={{0,8},{4,12},{8,0},{12,4},{16,24},{20,28},{24,16},{28,20},{1,9},{5... | collective-permute-start | bytes 6291464 | tf_op jit(solution)/shard_map/cond/branch_3_fun/ppermute | solution.py:197
  49.1 88.7 %collective-permute-start.48 = (bf16[32,32,1024]{2,1,0:T(8,128)(2,1)S(1)}, bf16[32,32,1024]{2,1,0:T(8,128)(2,1)S(1)}, u32[]{:S(2)}, u32[]{:S(2)}) collective-permute-start(bf16[32,32,1024]{2,1,0:T(8,128)(2,1)S(1)} %gather.108), channel_id=1, source_target_pairs={{0,16},{4,20},{8,24},{12,28},{16,0},{20,4},{24,8},{28,12},{1,17},{... | collective-permute-start | bytes 6291464 | tf_op jit(solution)/shard_map/cond/branch_3_fun/ppermute | solution.py:197
  90.8 157.3 %collective-permute-start.58 = (bf16[32,32,1024]{2,1,0:T(8,128)(2,1)S(1)}, bf16[32,32,1024]{2,1,0:T(8,128)(2,1)S(1)}, u32[]{:S(2)}, u32[]{:S(2)}) collective-permute-start(bf16[32,32,1024]{2,1,0:T(8,128)(2,1)S(1)} %gather.118), channel_id=1, source_target_pairs={{0,16},{4,20},{8,24},{12,28},{16,0},{20,4},{24,8},{28,12},{1,17},{... | collective-permute-start | bytes 6291464 | tf_op jit(solution)/shard_map/cond/branch_3_fun/ppermute | solution.py:197
  95.1 155.8 %collective-permute-start.55 = (bf16[32,32,1024]{2,1,0:T(8,128)(2,1)S(1)}, bf16[32,32,1024]{2,1,0:T(8,128)(2,1)S(1)}, u32[]{:S(2)}, u32[]{:S(2)}) collective-permute-start(bf16[32,32,1024]{2,1,0:T(8,128)(2,1)S(1)} %gather.115), channel_id=1, source_target_pairs={{0,8},{4,12},{8,0},{12,4},{16,24},{20,28},{24,16},{28,20},{1,9},{5... | collective-permute-start | bytes 6291464 | tf_op jit(solution)/shard_map/cond/branch_3_fun/ppermute | solution.py:197
  135.7 119.4 %collective-permute-start.52 = (bf16[32,32,1024]{2,1,0:T(8,128)(2,1)S(1)}, bf16[32,32,1024]{2,1,0:T(8,128)(2,1)S(1)}, u32[]{:S(2)}, u32[]{:S(2)}) collective-permute-start(bf16[32,32,1024]{2,1,0:T(8,128)(2,1)S(1)} %gather.112), channel_id=1, source_target_pairs={{0,16},{4,20},{8,24},{12,28},{16,0},{20,4},{24,8},{28,12},{1,17},{... | collective-permute-start | bytes 6291464 | tf_op jit(solution)/shard_map/cond/branch_3_fun/ppermute | solution.py:197
  140.0 119.4 %collective-permute-start.49 = (bf16[32,32,1024]{2,1,0:T(8,128)(2,1)S(1)}, bf16[32,32,1024]{2,1,0:T(8,128)(2,1)S(1)}, u32[]{:S(2)}, u32[]{:S(2)}) collective-permute-start(bf16[32,32,1024]{2,1,0:T(8,128)(2,1)S(1)} %gather.109), channel_id=1, source_target_pairs={{0,8},{4,12},{8,0},{12,4},{16,24},{20,28},{24,16},{28,20},{1,9},{5... | collective-permute-start | bytes 6291464 | tf_op jit(solution)/shard_map/cond/branch_3_fun/ppermute | solution.py:197
  143.7 100.5 %collective-permute-start.45 = (bf16[32,32,512]{2,1,0:T(8,128)(2,1)S(1)}, bf16[32,32,512]{2,1,0:T(8,128)(2,1)S(1)}, u32[]{:S(2)}, u32[]{:S(2)}) collective-permute-start(bf16[32,32,512]{2,1,0:T(8,128)(2,1)S(1)} %gather.105), channel_id=1, source_target_pairs={{0,8},{4,12},{8,0},{12,4},{16,24},{20,28},{24,16},{28,20},{1,9},{5... | collective-permute-start | bytes 3145736 | tf_op jit(solution)/shard_map/cond/branch_3_fun/ppermute | solution.py:197
  246.5 23.3 %collective-permute-start.46 = (bf16[32,32,512]{2,1,0:T(8,128)(2,1)S(1)}, bf16[32,32,512]{2,1,0:T(8,128)(2,1)S(1)}, u32[]{:S(2)}, u32[]{:S(2)}) collective-permute-start(bf16[32,32,512]{2,1,0:T(8,128)(2,1)S(1)} %gather.106), channel_id=1, source_target_pairs={{0,16},{4,20},{8,24},{12,28},{16,0},{20,4},{24,8},{28,12},{1,17},{... | collective-permute-start | bytes 3145736 | tf_op jit(solution)/shard_map/cond/branch_3_fun/ppermute | solution.py:197
  250.8 28.8 %collective-permute-start.59 = (bf16[32,32,1024]{2,1,0:T(8,128)(2,1)S(1)}, bf16[32,32,1024]{2,1,0:T(8,128)(2,1)S(1)}, u32[]{:S(2)}, u32[]{:S(2)}) collective-permute-start(bf16[32,32,1024]{2,1,0:T(8,128)(2,1)S(1)} %gather.119), channel_id=1, source_target_pairs={{0,4},{4,0},{8,12},{12,8},{16,20},{20,16},{24,28},{28,24},{1,5},{5... | collective-permute-start | bytes 6291464 | tf_op jit(solution)/shard_map/cond/branch_3_fun/ppermute | solution.py:197
  255.0 40.2 %collective-permute-start.56 = (bf16[32,32,1024]{2,1,0:T(8,128)(2,1)}, bf16[32,32,1024]{2,1,0:T(8,128)(2,1)S(1)}, u32[]{:S(2)}, u32[]{:S(2)}) collective-permute-start(bf16[32,32,1024]{2,1,0:T(8,128)(2,1)} %gather.116), channel_id=1, source_target_pairs={{0,4},{4,0},{8,12},{12,8},{16,20},{20,16},{24,28},{28,24},{1,5},{5... | collective-permute-start | bytes 6291464 | tf_op jit(solution)/shard_map/cond/branch_3_fun/ppermute | solution.py:197
  259.3 48.6 %collective-permute-start.53 = (bf16[32,32,1024]{2,1,0:T(8,128)(2,1)}, bf16[32,32,1024]{2,1,0:T(8,128)(2,1)S(1)}, u32[]{:S(2)}, u32[]{:S(2)}) collective-permute-start(bf16[32,32,1024]{2,1,0:T(8,128)(2,1)} %gather.113), channel_id=1, source_target_pairs={{0,4},{4,0},{8,12},{12,8},{16,20},{20,16},{24,28},{28,24},{1,5},{5... | collective-permute-start | bytes 6291464 | tf_op jit(solution)/shard_map/cond/branch_3_fun/ppermute | solution.py:197
  263.0 57.5 %collective-permute-start.50 = (bf16[32,32,1024]{2,1,0:T(8,128)(2,1)S(1)}, bf16[32,32,1024]{2,1,0:T(8,128)(2,1)S(1)}, u32[]{:S(2)}, u32[]{:S(2)}) collective-permute-start(bf16[32,32,1024]{2,1,0:T(8,128)(2,1)S(1)} %gather.110), channel_id=1, source_target_pairs={{0,4},{4,0},{8,12},{12,8},{16,20},{20,16},{24,28},{28,24},{1,5},{5... | collective-permute-start | bytes 6291464 | tf_op jit(solution)/shard_map/cond/branch_3_fun/ppermute | solution.py:197
  272.3 2.7 collective-permute-start.47
  279.7 1.3 copy-start
  281.0 1.6 copy-start.1

commit v3 on v2

--- a/solution.py
+++ b/solution.py
@@ -247,15 +247,33 @@
     return lists, jnp.max(jnp.stack(loads))
 
 
-def journey(rows, col, width, lists, cap, bits, sentences):
-    sources, cols = [rows], [col]
-    bases = tuple(n * sentences for n in range(4))
-    for hop, bit in enumerate((*bits, 1)):
-        sent = gather(
-            lists[hop, :cap], sources, tuple(cols), bases[: len(sources)], width
+class Journey:
+    def __init__(self, rows, col, width, lists, cap, bits, sentences):
+        self.sources, self.cols, self.width = [rows], [col], width
+        self.lists, self.cap, self.bits = lists, cap, (*bits, 1)
+        self.bases = tuple(n * sentences for n in range(4))
+
+    def collect(self):
+        hop = len(self.sources) - 1
+        self.sent = gather(
+            self.lists[hop, : self.cap],
+            self.sources,
+            tuple(self.cols),
+            self.bases[: hop + 1],
+            self.width,
         )
-        sources, cols = sources + [flip(sent, bit)], cols + [0]
-    return sources, tuple(cols), bases
+
+    def hop(self):
+        self.collect()
+        self.travel()
+
+    def travel(self):
+        bit = self.bits[len(self.sources) - 1]
+        self.sources = self.sources + [flip(self.sent, bit)]
+        self.cols = self.cols + [0]
+
+    def got(self):
+        return self.sources, tuple(self.cols), self.bases
 
 
 def per_device(queries, key_rows, value_rows, destination, token_count, doc_ids):
@@ -277,10 +295,11 @@
     def split(rows):
         return rows.reshape(rows.shape[0], slot_len, ways, kv_width)
 
-    kv = jnp.concatenate([split(key_rows), split(value_rows)], axis=3)
-    kv = lax.all_to_all(
-        jnp.transpose(kv, (2, 0, 1, 3)), "tensor", split_axis=0, concat_axis=0, tiled=True
-    ).reshape(sentences, slot_len, 2 * kv_width)
+    def own_heads(key_rows, value_rows):
+        kv = jnp.concatenate([split(key_rows), split(value_rows)], axis=3)
+        return lax.all_to_all(
+            jnp.transpose(kv, (2, 0, 1, 3)), "tensor", split_axis=0, concat_axis=0, tiled=True
+        ).reshape(sentences, slot_len, 2 * kv_width)
 
     dest = table[:, 0, :].reshape(-1)
     counts = table[:, 1, :].reshape(-1)
@@ -319,17 +338,10 @@
 
     chunks = q_width // chunk_width
 
-    def attend_all(got_kv, kv_codes, got_q, q_codes):
-        keys, values = pack(kv_codes, first, pick, *got_kv, kv_local)
-        out = None
-        turn = sorted(range(chunks), key=lambda n: (n % (chunks // 2 or 1), n))
-        for chunk in turn:
-            kv_head = chunk * heads // per_group
-            out = attend(
-                q_codes[chunk], first, keys, values, pick, bias, *got_q[chunk], out, chunk, heads,
-                kv_head, q_width,
-            )
-        return out
+    def attend_one(chunk, kv_packed, first, got, codes, out):
+        return attend(
+            codes, first, *kv_packed, pick, bias, *got, out, chunk, heads, chunk * heads // per_group, q_width
+        )
 
     if groups != 8:
         capacity = max(2, (2 * sentences + groups - 1) // groups)
@@ -348,32 +360,86 @@
             got = lax.all_to_all(sent, "dp", split_axis=0, concat_axis=0, tiled=True)
             return [got], (0,), (0,)
 
-        got_kv = exchange(kv, 0, 2 * kv_width)
+        got_kv = exchange(own_heads(key_rows, value_rows), 0, 2 * kv_width)
         got_q = [exchange(queries, n * chunk_width, chunk_width) for n in range(chunks)]
-        return attend_all(got_kv, codes, got_q, [codes] * chunks)
+        kv_packed = pack(codes, first, pick, *got_kv, kv_local)
+        out = None
+        for n in range(chunks):
+            out = attend_one(n, kv_packed, first, got_q[n], codes, out)
+        return out
 
     bits = ((2, 4), (4, 2))
     tables, loads = zip(
         *(hop_tables(dest, source, lane, me, groups, sentences, *pair) for pair in bits)
     )
     most = jnp.maximum(*loads)
-    caps = sorted({min(sentences, n) for n in (20, 22, 25, sentences)})
-
-    def with_cap(cap, queries, kv, *tables):
-        got_q = []
-        for n in range(chunks):
-            half = n * 2 // chunks
-            got_q.append(
-                journey(queries, n * chunk_width, chunk_width, tables[half], cap, bits[half], sentences)
+    caps = sorted({min(sentences, n) for n in (21, 23, 25, sentences)})
+
+    def with_cap(cap, queries, key_rows, value_rows, *tables):
+        halves = len(tables)
+
+        def start(n, half):
+            return Journey(
+                queries, n * chunk_width, chunk_width, tables[half], cap, bits[half], sentences
             )
-        got_kv = journey(kv, 0, 2 * kv_width, tables[0], cap, bits[0], sentences)
-        return attend_all(
-            got_kv, tables[0][3], got_q, [tables[n * 2 // chunks][3] for n in range(chunks)]
+
+        per_half = chunks // halves
+        rounds = [
+            [start(half * per_half + n, half) for half in range(halves)] for n in range(per_half)
+        ]
+        for one in rounds[0]:
+            one.hop()
+        kv = Journey(
+            own_heads(key_rows, value_rows), 0, 2 * kv_width, tables[0], cap, bits[0], sentences
         )
+        kv.hop()
+        ready = kv.sources[-1]
+        flow_first, kv_packed, out = first, None, None
+        for n in range(per_half):
+            following = rounds[n + 1] if n + 1 < per_half else []
+            if following:
+                ready, *held = lax.optimization_barrier(
+                    (ready, *(one.lists for one in following))
+                )
+                if n == 0:
+                    kv.sources[-1] = ready
+                for one, lists in zip(following, held):
+                    one.lists = lists
+                    one.hop()
+            for one in rounds[n]:
+                if n == 0:
+                    one.hop()
+            if n == 0:
+                kv.hop()
+            for one in rounds[n]:
+                one.hop()
+            if n == 0:
+                kv.hop()
+            if following:
+                for one in following:
+                    one.collect()
+                flow_first, *sent = lax.optimization_barrier(
+                    (first, *(one.sent for one in following))
+                )
+                for one, rows in zip(following, sent):
+                    one.sent = rows
+                    one.travel()
+            if n == 0:
+                kv_packed = pack(tables[0][3], flow_first, pick, *kv.got(), kv_local)
+            for half, one in enumerate(rounds[n]):
+                out = attend_one(
+                    half * per_half + n, kv_packed, flow_first, one.got(), tables[half][3], out
+                )
+            if following:
+                out, *held = lax.optimization_barrier((out, *(one.lists for one in following)))
+                for one, lists in zip(following, held):
+                    one.lists = lists
+                ready, flow_first = out, first
+        return out
 
     tier = sum((most > cap).astype(jnp.int32) for cap in caps[:-1])
     return lax.switch(
-        tier, [functools.partial(with_cap, cap) for cap in caps], queries, kv, *tables
+        tier, [functools.partial(with_cap, cap) for cap in caps], queries, key_rows, value_rows, *tables
     )
 
 

time: 338 us -> 223 us (0.66); the launches traced: 334 us -> 227 us
  waiting for transfers between devices: 191 us -> 89.8 us
  starting transfers between devices: 21.8 us -> 17.9 us
    ppermute x15, waiting for transfers between devices: 185 us -> 72.3 us  [flip(): return lax.ppermute(rows, 'dp', pairs)]
    all_to_all x1, waiting for transfers between devices: 6.43 us -> 17.5 us  [own_heads(): lax.all_to_all(jnp.transpose(kv, (2, 0, 1, 3)), 'tensor', split_axis=0, c...]
    pallas_call x15, Pallas kernels: 36.4 us -> 31.3 us  [gather(): pl.pallas_call(functools.partial(gather_kernel, cols=cols, bases=bases),...]
  transfers between devices with their start and end apart: 16 -> 16, of which waited for: 6 -> 8; matrix products, arithmetic and copies ran while one was open for 2% -> 1% of each run, Pallas kernels for 23% -> 33%
where the time goes in v3:
time: 223 us; the launch traced here: 227 us
  waiting for transfers between devices  89.8 us (40%)
  Pallas kernels  88.9 us (40%)
  starting transfers between devices  17.9 us (8%)
  blocking collectives  10.3 us (5%)
  other arithmetic  7.91 us (4%)
  local copies, waits for them, and re-layouts  4.91 us (2%)
  between operations  4.35 us (2%)
    ppermute x15, waiting for transfers between devices, flip(): return lax.ppermute(rows, 'dp', pairs)  72.3 us
    pallas_call x4, Pallas kernels, attend(): pl.pallas_call(functools.partial(attend_kernel, cols=cols, bases=bases, h...  53 us
    pallas_call x15, Pallas kernels, gather(): pl.pallas_call(functools.partial(gather_kernel, cols=cols, bases=bases),...  31.3 us
    all_to_all x1, waiting for transfers between devices, own_heads(): lax.all_to_all(jnp.transpose(kv, (2, 0, 1, 3)), 'tensor', split_axis=0, c...  17.5 us
    ppermute x15, starting transfers between devices, flip(): return lax.ppermute(rows, 'dp', pairs)  13 us
    all_gather x1, blocking collectives, per_device(): table = lax.all_gather(jnp.stack([destination, token_count]), 'dp', axis=0)  10.3 us
    all_to_all x1, starting transfers between devices, own_heads(): lax.all_to_all(jnp.transpose(kv, (2, 0, 1, 3)), 'tensor', split_axis=0, c...  4.87 us
    pallas_call x1, Pallas kernels, pack(): pl.pallas_call(functools.partial(pack_kernel, cols=cols, bases=bases), gr...  4.61 us
  transfers between devices with their start and end apart: 16, of which 8 were waited for; matrix products, arithmetic and copies ran while one was open for 1% of the time, Pallas kernels for 33%

profile of v3, /device:TPU:0, one launch (start us, length us, event | category | flops | bytes accessed | tf_op | source)
XLA Modules:
  0.0 227.1 jit_solution(15758236633805676253)
XLA Ops:
  2.4 10.3 %all-gather.1 = s32[8,2,32]{2,1,0:T(2,128)S(1)} all-gather(s32[1,2,32]{2,1,0:T(2,128)S(1)} %add_bitcast_fusion), channel_id=2, replica_groups=mesh['dp'=8,'tensor'=4] {'dp'}, dimensions={0}, use_global_device_ids=true | all-gather | bytes 2304 | tf_op jit(solution)/shard_map/all_gather | solution.py:293
  26.4 200.5 %conditional.1 = (bf16[1024,4096]{1,0:T(8,128)(2,1)}) conditional(s32[]{:T(128)} %clamp.3, (pred[4,256]{1,0:T(4,128)(4,1)}, pred[4,256]{1,0:T(4,128)(4,1)S(1)}, bf16[8,32,1024]{2,1,0:T(8,128)(2,1)S(1)}, bf16[8,32,1024]{2,1,0:T(8,128)(2,1)S(1)}, bf16[32,32,4096]{2,1,0:T(8,128)(2,1)}, /*index=5*/s32[8]{0:T(128)}, ...), branch_computations={%region_19.20_spmd, %region_20.21_spmd, %region_21.22_spmd, %regio... | conditional | flops 6446379008 | bytes 278932320 | solution.py:441
  27.6 4.9 %all-to-all-start.1 = ((bf16[4,8,32,512]{3,2,1,0:T(8,128)(2,1)}), bf16[4,8,32,512]{3,2,1,0:T(8,128)(2,1)S(1)}, u32[]{:S(2)}, u32[]{:S(2)}) async-start(bf16[4,8,32,512]{3,2,1,0:T(8,128)(2,1)} %maximum_bitcast_fusion.1), calls=%async_computation.1 | async-start | bytes 2097152 | tf_op jit(solution)/shard_map/cond/branch_1_fun/all_to_all | solution.py:300
  32.9 3.3 %gather.85 = bf16[23,32,1024]{2,1,0:T(8,128)(2,1)} custom-call(s32[23]{0:T(128)S(1)} %get-tuple-element.741.code_ref, bf16[32,32,4096]{2,1,0:T(8,128)(2,1)} %get-tuple-element.224.rest_0_), custom_call_target="tpu_custom_call" | custom-call | bytes 3014656 | tf_op jit(solution)/shard_map/cond/branch_1_fun/gather/pallas_call | solution.py:52
  36.2 1.7 collective-permute-start.24
  38.1 2.4 %gather.82 = bf16[23,32,1024]{2,1,0:T(8,128)(2,1)} custom-call(s32[23]{0:T(128)S(1)} %get-tuple-element.738.code_ref, bf16[32,32,4096]{2,1,0:T(8,128)(2,1)S(1)} %copy-done.3), custom_call_target="tpu_custom_call" | custom-call | bytes 3014656 | tf_op jit(solution)/shard_map/cond/branch_1_fun/gather/pallas_call | solution.py:52
  41.3 17.5 %all-to-all-done.1 = bf16[4,8,32,512]{3,2,1,0:T(8,128)(2,1)S(1)} async-done(((bf16[4,8,32,512]{3,2,1,0:T(8,128)(2,1)}), bf16[4,8,32,512]{3,2,1,0:T(8,128)(2,1)S(1)}, u32[]{:S(2)}, u32[]{:S(2)}) %all-to-all-start.1) | async-done | bytes 1048608 | tf_op jit(solution)/shard_map/cond/branch_1_fun/all_to_all | solution.py:300
  58.7 1.7 gather.75
  62.0 10.4 %collective-permute-done.24.rest_1_ = bf16[23,32,1024]{2,1,0:T(8,128)(2,1)} collective-permute-done((bf16[23,32,1024]{2,1,0:T(8,128)(2,1)}, bf16[23,32,1024]{2,1,0:T(8,128)(2,1)}, u32[]{:S(2)}, u32[]{:S(2)}) %collective-permute-start.24) | collective-permute-done | bytes 1507360 | tf_op jit(solution)/shard_map/cond/branch_1_fun/ppermute | solution.py:197
  72.4 2.2 gather.86
  76.2 2.7 %gather.83 = bf16[23,32,1024]{2,1,0:T(8,128)(2,1)S(1)} custom-call(s32[23]{0:T(128)S(1)} %get-tuple-element.737.code_ref, bf16[32,32,4096]{2,1,0:T(8,128)(2,1)} %get-tuple-element.224.rest_0_, bf16[23,32,1024]{2,1,0:T(8,128)(2,1)S(1)} %collective-permute-done.21.rest_1_), custom_call_target="tpu_custom_call" | custom-call | bytes 3014656 | tf_op jit(solution)/shard_map/cond/branch_1_fun/gather/pallas_call | solution.py:52
  79.6 8.8 %collective-permute-done.15.rest_1_ = bf16[23,32,512]{2,1,0:T(8,128)(2,1)S(1)} collective-permute-done((bf16[23,32,512]{2,1,0:T(8,128)(2,1)S(1)}, bf16[23,32,512]{2,1,0:T(8,128)(2,1)S(1)}, u32[]{:S(2)}, u32[]{:S(2)}) %collective-permute-start.15) | collective-permute-done | bytes 753696 | tf_op jit(solution)/shard_map/cond/branch_1_fun/ppermute | solution.py:197
  89.7 1.7 collective-permute-start.16
  93.1 1.9 gather.80
  95.0 1.7 collective-permute-start.18
  96.7 13.9 %collective-permute-done.25.rest_2_ = bf16[23,32,1024]{2,1,0:T(8,128)(2,1)S(1)} collective-permute-done((bf16[23,32,1024]{2,1,0:T(8,128)(2,1)S(1)}, bf16[23,32,1024]{2,1,0:T(8,128)(2,1)S(1)}, u32[]{:S(2)}, u32[]{:S(2)}) %collective-permute-start.25) | collective-permute-done | bytes 1507360 | tf_op jit(solution)/shard_map/cond/branch_1_fun/ppermute | solution.py:197
  110.6 2.0 gather.87
  112.7 8.0 %collective-permute-done.22.rest_2_ = bf16[23,32,1024]{2,1,0:T(8,128)(2,1)S(1)} collective-permute-done((bf16[23,32,1024]{2,1,0:T(8,128)(2,1)S(1)}, bf16[23,32,1024]{2,1,0:T(8,128)(2,1)S(1)}, u32[]{:S(2)}, u32[]{:S(2)}) %collective-permute-start.22) | collective-permute-done | bytes 1507360 | tf_op jit(solution)/shard_map/cond/branch_1_fun/ppermute | solution.py:197
  120.7 2.4 %gather.84 = bf16[23,32,1024]{2,1,0:T(8,128)(2,1)S(1)} custom-call(s32[23]{0:T(128)S(1)} %get-tuple-element.736.code_ref, bf16[32,32,4096]{2,1,0:T(8,128)(2,1)S(1)} %bitcast.251, bf16[23,32,1024]{2,1,0:T(8,128)(2,1)S(1)} %collective-permute-done.21.rest_1_, bf16[23,32,1024]{2,1,0:T(8,128)(2,1)S(1)} %collective-permute-done.22.rest_2_), custom_call_target="tpu_custom_call" | custom-call | bytes 3014656 | tf_op jit(solution)/shard_map/cond/branch_1_fun/gather/pallas_call | solution.py:52
  123.2 29.0 %collective-permute-done.16.rest_1_ = bf16[23,32,1024]{2,1,0:T(8,128)(2,1)S(1)} collective-permute-done((bf16[23,32,1024]{2,1,0:T(8,128)(2,1)S(1)}, bf16[23,32,1024]{2,1,0:T(8,128)(2,1)S(1)}, u32[]{:S(2)}, u32[]{:S(2)}) %collective-permute-start.16) | collective-permute-done | bytes 1507360 | tf_op jit(solution)/shard_map/cond/branch_1_fun/ppermute | solution.py:197
  152.2 1.7 gather.77
  153.9 1.8 gather.79
  155.8 2.1 collective-permute-start.28
  157.9 2.0 gather.81
  160.6 1.6 collective-permute-done.19.rest_3_
  162.2 4.6 %pack.5 = (bf16[2,1280,128]{2,1,0:T(8,128)(2,1)S(1)}, bf16[2,1280,128]{2,1,0:T(8,128)(2,1)S(1)}) custom-call(s32[32]{0:T(128)S(1)} %slice_bitcast_fusion.26.code_ref, s32[8]{0:T(128)S(1)} %copy-done.26, bf16[1024,288]{1,0:T(8,128)(2,1)S(1)} %copy-done.6, bf16[32,32,512]{2,1,0:T(8,128)(2,1)S(1)} %bitcast.239, ...), custom_call_target="tpu_custom_call" | custom-call | tf_op jit(solution)/shard_map/cond/branch_1_fun/pack/pallas_call | solution.py:95
  166.9 13.9 %attend.20.rest_4_ = bf16[1024,4096]{1,0:T(8,128)(2,1)} custom-call(s32[32]{0:T(128)S(1)} %slice_bitcast_fusion.26.code_ref, s32[8]{0:T(128)S(1)} %copy-done.26, bf16[2,1280,128]{2,1,0:T(8,128)(2,1)S(1)} %get-tuple-element.104.k_ref, bf16[2,1280,128]{2,1,0:T(8,128)(2,1)S(1)} %get-tuple-element.105.v_ref, bf16[1024,288]{1,0:T(8,128)(2,1)} %copy-done.5, ...), custom_call_target="tpu_custom_call" | custom-call | flops 1610612736 | bytes 6291456 | tf_op jit(solution)/shard_map/cond/branch_1_fun/attend/pallas_call | solution.py:170
  180.8 13.0 %attend.21.rest_4_ = bf16[1024,4096]{1,0:T(8,128)(2,1)} custom-call(s32[32]{0:T(128)S(1)} %slice_bitcast_fusion.27.code_ref, s32[8]{0:T(128)S(1)} %copy-done.26, bf16[2,1280,128]{2,1,0:T(8,128)(2,1)S(1)} %get-tuple-element.104.k_ref, bf16[2,1280,128]{2,1,0:T(8,128)(2,1)S(1)} %get-tuple-element.105.v_ref, ...), custom_call_target="tpu_custom_call", output_to_operand_aliasing={{}: (10, {})} | custom-call | flops 1610612736 | bytes 6291456 | tf_op jit(solution)/shard_map/cond/branch_1_fun/attend/pallas_call | solution.py:170
  194.5 2.4 %gather.89 = bf16[23,32,1024]{2,1,0:T(8,128)(2,1)S(1)} custom-call(s32[23]{0:T(128)S(1)} %slice_bitcast_fusion.14.code_ref, bf16[32,32,4096]{2,1,0:T(8,128)(2,1)S(1)} %bitcast.251, bf16[23,32,1024]{2,1,0:T(8,128)(2,1)S(1)} %collective-permute-done.16.rest_1_, bf16[23,32,1024]{2,1,0:T(8,128)(2,1)S(1)} %collective-permute-done.28.rest_2_), custom_call_target="tpu_custom_call" | custom-call | bytes 3014656 | tf_op jit(solution)/shard_map/cond/branch_1_fun/gather/pallas_call | solution.py:52
  197.0 2.4 %gather.88 = bf16[23,32,1024]{2,1,0:T(8,128)(2,1)S(1)} custom-call(s32[23]{0:T(128)S(1)} %slice_bitcast_fusion.15.code_ref, bf16[32,32,4096]{2,1,0:T(8,128)(2,1)S(1)} %bitcast.251, bf16[23,32,1024]{2,1,0:T(8,128)(2,1)S(1)} %collective-permute-done.17.rest_1_, bf16[23,32,1024]{2,1,0:T(8,128)(2,1)S(1)} %collective-permute-done.20.rest_2_), custom_call_target="tpu_custom_call" | custom-call | bytes 3014656 | tf_op jit(solution)/shard_map/cond/branch_1_fun/gather/pallas_call | solution.py:52
  200.3 13.0 %attend.22.rest_4_ = bf16[1024,4096]{1,0:T(8,128)(2,1)} custom-call(s32[32]{0:T(128)S(1)} %slice_bitcast_fusion.26.code_ref, s32[8]{0:T(128)S(1)} %copy-done.26, bf16[2,1280,128]{2,1,0:T(8,128)(2,1)S(1)} %get-tuple-element.104.k_ref, bf16[2,1280,128]{2,1,0:T(8,128)(2,1)S(1)} %get-tuple-element.105.v_ref, ...), custom_call_target="tpu_custom_call", output_to_operand_aliasing={{}: (10, {})} | custom-call | flops 1610612736 | bytes 6291456 | tf_op jit(solution)/shard_map/cond/branch_1_fun/attend/pallas_call | solution.py:170
  213.3 13.0 %attend.23 = bf16[1024,4096]{1,0:T(8,128)(2,1)} custom-call(s32[32]{0:T(128)S(1)} %slice_bitcast_fusion.27.code_ref, s32[8]{0:T(128)S(1)} %copy-done.26, bf16[2,1280,128]{2,1,0:T(8,128)(2,1)S(1)} %get-tuple-element.104.k_ref, bf16[2,1280,128]{2,1,0:T(8,128)(2,1)S(1)} %get-tuple-element.105.v_ref, ...), custom_call_target="tpu_custom_call", output_to_operand_aliasing={{}: (10, {})} | custom-call | flops 1610612736 | bytes 6291456 | tf_op jit(solution)/shard_map/cond/branch_1_fun/attend/pallas_call | solution.py:170
  (147 shorter events, 23.6 us)
Async XLA Ops:
  0.0 26.3 %copy-start.15 = (bf16[8,32,1024]{2,1,0:T(8,128)(2,1)S(1)}, bf16[8,32,1024]{2,1,0:T(8,128)(2,1)}, u32[]{:S(2)}) copy-start(bf16[8,32,1024]{2,1,0:T(8,128)(2,1)} %param.12) | copy-start | bytes 1572868
  0.0 26.3 %copy-start.14 = (bf16[8,32,1024]{2,1,0:T(8,128)(2,1)S(1)}, bf16[8,32,1024]{2,1,0:T(8,128)(2,1)}, u32[]{:S(2)}) copy-start(bf16[8,32,1024]{2,1,0:T(8,128)(2,1)} %param.11) | copy-start | bytes 1572868
  13.6 11.2 %copy-start.24 = (s32[8]{0:T(128)}, s32[8]{0:T(128)S(1)}, u32[]{:S(2)}) copy-start(s32[8]{0:T(128)S(1)} %broadcast_minimum_fusion) | copy-start | bytes 100
  27.6 31.1 %all-to-all-start.1 = ((bf16[4,8,32,512]{3,2,1,0:T(8,128)(2,1)}), bf16[4,8,32,512]{3,2,1,0:T(8,128)(2,1)S(1)}, u32[]{:S(2)}, u32[]{:S(2)}) async-start(bf16[4,8,32,512]{3,2,1,0:T(8,128)(2,1)} %maximum_bitcast_fusion.1), calls=%async_computation.1 | async-start | bytes 2097152 | tf_op jit(solution)/shard_map/cond/branch_1_fun/all_to_all | solution.py:300
  32.8 127.8 %copy-start.66 = (s32[4,32]{1,0:T(4,128)}, s32[4,32]{1,0:T(4,128)S(1)}, u32[]{:S(2)}) copy-start(s32[4,32]{1,0:T(4,128)S(1)} %select_reduce_fusion.2) | copy-start | bytes 1540 | tf_op jit(solution)/shard_map/cond
  32.8 5.1 %copy-start.38 = (s32[3,256]{1,0:T(4,128)S(1)}, s32[3,256]{1,0:T(4,128)}, u32[]{:S(2)}) copy-start(s32[3,256]{1,0:T(4,128)} %get-tuple-element.657) | copy-start | bytes 9220 | tf_op jit(solution)/shard_map/cond
  32.8 5.0 %copy-start.56 = (pred[3,256]{1,0:T(4,128)(4,1)S(1)}, pred[3,256]{1,0:T(4,128)(4,1)}, u32[]{:S(2)}) copy-start(pred[3,256]{1,0:T(4,128)(4,1)} %get-tuple-element.610) | copy-start | bytes 2308 | tf_op jit(solution)/shard_map/cond
  32.8 5.1 %copy-start.34 = (s32[4,256]{1,0:T(4,128)S(1)}, s32[4,256]{1,0:T(4,128)}, u32[]{:S(2)}) copy-start(s32[4,256]{1,0:T(4,128)} %get-tuple-element.385) | copy-start | bytes 12292 | tf_op jit(solution)/shard_map/cond
  32.8 5.1 %copy-start.51 = (pred[4,256]{1,0:T(4,128)(4,1)S(1)}, pred[4,256]{1,0:T(4,128)(4,1)}, u32[]{:S(2)}) copy-start(pred[4,256]{1,0:T(4,128)(4,1)} %get-tuple-element.326) | copy-start | bytes 3076 | tf_op jit(solution)/shard_map/cond
  32.8 5.1 %copy-start.60 = (s32[256]{0:T(256)S(1)}, s32[256]{0:T(256)}, u32[]{:S(2)}) copy-start(s32[256]{0:T(256)} %get-tuple-element.506) | copy-start | bytes 3076 | tf_op jit(solution)/shard_map/cond
  32.9 5.2 %copy-start.3 = (bf16[32,32,4096]{2,1,0:T(8,128)(2,1)S(1)}, bf16[32,32,4096]{2,1,0:T(8,128)(2,1)}, u32[]{:S(2)}) copy-start(bf16[32,32,4096]{2,1,0:T(8,128)(2,1)} %get-tuple-element.224.rest_0_) | copy-start | bytes 25165828 | tf_op jit(solution)/shard_map/cond
  36.2 36.2 %collective-permute-start.24 = (bf16[23,32,1024]{2,1,0:T(8,128)(2,1)}, bf16[23,32,1024]{2,1,0:T(8,128)(2,1)}, u32[]{:S(2)}, u32[]{:S(2)}) collective-permute-start(bf16[23,32,1024]{2,1,0:T(8,128)(2,1)} %gather.85), channel_id=1, source_target_pairs={{0,8},{4,12},{8,0},{12,4},{16,24},{20,28},{24,16},{28,20},{1,9},{5... | collective-permute-start | bytes 4521992 | tf_op jit(solution)/shard_map/cond/branch_1_fun/ppermute | solution.py:197
  40.5 35.7 %collective-permute-start.21 = (bf16[23,32,1024]{2,1,0:T(8,128)(2,1)}, bf16[23,32,1024]{2,1,0:T(8,128)(2,1)S(1)}, u32[]{:S(2)}, u32[]{:S(2)}) collective-permute-start(bf16[23,32,1024]{2,1,0:T(8,128)(2,1)} %gather.82), channel_id=1, source_target_pairs={{0,16},{4,20},{8,24},{12,28},{16,0},{20,4},{24,8},{28,12},{1,17},{... | collective-permute-start | bytes 4521992 | tf_op jit(solution)/shard_map/cond/branch_1_fun/ppermute | solution.py:197
  60.4 28.0 %collective-permute-start.15 = (bf16[23,32,512]{2,1,0:T(8,128)(2,1)S(1)}, bf16[23,32,512]{2,1,0:T(8,128)(2,1)S(1)}, u32[]{:S(2)}, u32[]{:S(2)}) collective-permute-start(bf16[23,32,512]{2,1,0:T(8,128)(2,1)S(1)} %gather.75), channel_id=1, source_target_pairs={{0,8},{4,12},{8,0},{12,4},{16,24},{20,28},{24,16},{28,20},{1,9},{5... | collective-permute-start | bytes 2261000 | tf_op jit(solution)/shard_map/cond/branch_1_fun/ppermute | solution.py:197
  72.4 16.1 %slice-start.2 = ((s8[8388608]{0:T(1024)(128)(4,1)}), s8[4194304]{0:T(1024)(128)(4,1)S(1)}, s32[]{:S(2)}) async-start(s8[8388608]{0:T(1024)(128)(4,1)} %bitcast.250), calls=%async_computation.6 | async-start | bytes 8388608 | tf_op jit(solution)/shard_map/cond
  74.6 36.0 %collective-permute-start.25 = (bf16[23,32,1024]{2,1,0:T(8,128)(2,1)S(1)}, bf16[23,32,1024]{2,1,0:T(8,128)(2,1)S(1)}, u32[]{:S(2)}, u32[]{:S(2)}) collective-permute-start(bf16[23,32,1024]{2,1,0:T(8,128)(2,1)S(1)} %gather.86), channel_id=1, source_target_pairs={{0,16},{4,20},{8,24},{12,28},{16,0},{20,4},{24,8},{28,12},{1,17},{... | collective-permute-start | bytes 4521992 | tf_op jit(solution)/shard_map/cond/branch_1_fun/ppermute | solution.py:197
  76.2 12.3 %slice-start.3 = ((s8[8388608]{0:T(1024)(128)(4,1)}), s8[4194304]{0:T(1024)(128)(4,1)S(1)}, s32[]{:S(2)}) async-start(s8[8388608]{0:T(1024)(128)(4,1)} %bitcast.250), calls=%async_computation.7 | async-start | bytes 8388608 | tf_op jit(solution)/shard_map/cond
  78.9 41.8 %collective-permute-start.22 = (bf16[23,32,1024]{2,1,0:T(8,128)(2,1)S(1)}, bf16[23,32,1024]{2,1,0:T(8,128)(2,1)S(1)}, u32[]{:S(2)}, u32[]{:S(2)}) collective-permute-start(bf16[23,32,1024]{2,1,0:T(8,128)(2,1)S(1)} %gather.83), channel_id=1, source_target_pairs={{0,8},{4,12},{8,0},{12,4},{16,24},{20,28},{24,16},{28,20},{1,9},{5... | collective-permute-start | bytes 4521992 | tf_op jit(solution)/shard_map/cond/branch_1_fun/ppermute | solution.py:197
  89.7 62.5 %collective-permute-start.16 = (bf16[23,32,1024]{2,1,0:T(8,128)(2,1)S(1)}, bf16[23,32,1024]{2,1,0:T(8,128)(2,1)S(1)}, u32[]{:S(2)}, u32[]{:S(2)}) collective-permute-start(bf16[23,32,1024]{2,1,0:T(8,128)(2,1)S(1)} %gather.76), channel_id=1, source_target_pairs={{0,8},{4,12},{8,0},{12,4},{16,24},{20,28},{24,16},{28,20},{1,9},{5... | collective-permute-start | bytes 4521992 | tf_op jit(solution)/shard_map/cond/branch_1_fun/ppermute | solution.py:197
  92.7 61.3 %collective-permute-start.17 = (bf16[23,32,1024]{2,1,0:T(8,128)(2,1)S(1)}, bf16[23,32,1024]{2,1,0:T(8,128)(2,1)S(1)}, u32[]{:S(2)}, u32[]{:S(2)}) collective-permute-start(bf16[23,32,1024]{2,1,0:T(8,128)(2,1)S(1)} %gather.78), channel_id=1, source_target_pairs={{0,16},{4,20},{8,24},{12,28},{16,0},{20,4},{24,8},{28,12},{1,17},{... | collective-permute-start | bytes 4521992 | tf_op jit(solution)/shard_map/cond/branch_1_fun/ppermute | solution.py:197
  95.0 62.9 %collective-permute-start.18 = (bf16[23,32,512]{2,1,0:T(8,128)(2,1)S(1)}, bf16[23,32,512]{2,1,0:T(8,128)(2,1)S(1)}, u32[]{:S(2)}, u32[]{:S(2)}) collective-permute-start(bf16[23,32,512]{2,1,0:T(8,128)(2,1)S(1)} %gather.80), channel_id=1, source_target_pairs={{0,16},{4,20},{8,24},{12,28},{16,0},{20,4},{24,8},{28,12},{1,17},{... | collective-permute-start | bytes 2261000 | tf_op jit(solution)/shard_map/cond/branch_1_fun/ppermute | solution.py:197
  112.6 54.3 %collective-permute-start.26 = (bf16[23,32,1024]{2,1,0:T(8,128)(2,1)S(1)}, bf16[23,32,1024]{2,1,0:T(8,128)(2,1)S(1)}, u32[]{:S(2)}, u32[]{:S(2)}) collective-permute-start(bf16[23,32,1024]{2,1,0:T(8,128)(2,1)S(1)} %gather.87), channel_id=1, source_target_pairs={{0,4},{4,0},{8,12},{12,8},{16,20},{20,16},{24,28},{28,24},{1,5},{5... | collective-permute-start | bytes 4521992 | tf_op jit(solution)/shard_map/cond/branch_1_fun/ppermute | solution.py:197
  123.1 57.7 %collective-permute-start.23 = (bf16[23,32,1024]{2,1,0:T(8,128)(2,1)S(1)}, bf16[23,32,1024]{2,1,0:T(8,128)(2,1)S(1)}, u32[]{:S(2)}, u32[]{:S(2)}) collective-permute-start(bf16[23,32,1024]{2,1,0:T(8,128)(2,1)S(1)} %gather.84), channel_id=1, source_target_pairs={{0,4},{4,0},{8,12},{12,8},{16,20},{20,16},{24,28},{28,24},{1,5},{5... | collective-permute-start | bytes 4521992 | tf_op jit(solution)/shard_map/cond/branch_1_fun/ppermute | solution.py:197
  155.7 4.4 %copy-start.42 = (s32[384]{0:T(512)S(1)}, s32[384]{0:T(512)}, u32[]{:S(2)}) copy-start(s32[384]{0:T(512)} %get-tuple-element.557) | copy-start | bytes 4612 | tf_op jit(solution)/shard_map/cond
  155.7 4.4 %copy-start.17 = (s32[8,384]{1,0:T(8,128)S(1)}, s32[8,384]{1,0:T(8,128)}, u32[]{:S(2)}) copy-start(s32[8,384]{1,0:T(8,128)} %get-tuple-element.444) | copy-start | bytes 36868 | tf_op jit(solution)/shard_map/cond
  155.8 4.4 %copy-start.30 = (s32[1024]{0:T(1024)S(1)}, s32[1024]{0:T(1024)}, u32[]{:S(2)}) copy-start(s32[1024]{0:T(1024)} %get-tuple-element.380) | copy-start | bytes 12292 | tf_op jit(solution)/shard_map/cond
  155.8 38.8 %collective-permute-start.28 = (bf16[23,32,1024]{2,1,0:T(8,128)(2,1)S(1)}, bf16[23,32,1024]{2,1,0:T(8,128)(2,1)S(1)}, u32[]{:S(2)}, u32[]{:S(2)}) collective-permute-start(bf16[23,32,1024]{2,1,0:T(8,128)(2,1)S(1)} %gather.77), channel_id=1, source_target_pairs={{0,16},{4,20},{8,24},{12,28},{16,0},{20,4},{24,8},{28,12},{1,17},{... | collective-permute-start | bytes 4521992 | tf_op jit(solution)/shard_map/cond/branch_1_fun/ppermute | solution.py:197
  159.9 2.3 %collective-permute-start.19 = (bf16[23,32,512]{2,1,0:T(8,128)(2,1)S(1)}, bf16[23,32,512]{2,1,0:T(8,128)(2,1)S(1)}, u32[]{:S(2)}, u32[]{:S(2)}) collective-permute-start(bf16[23,32,512]{2,1,0:T(8,128)(2,1)S(1)} %gather.81), channel_id=1, source_target_pairs={{0,4},{4,0},{8,12},{12,8},{16,20},{20,16},{24,28},{28,24},{1,5},{5... | collective-permute-start | bytes 2261000 | tf_op jit(solution)/shard_map/cond/branch_1_fun/ppermute | solution.py:197
  160.0 37.0 %collective-permute-start.20 = (bf16[23,32,1024]{2,1,0:T(8,128)(2,1)S(1)}, bf16[23,32,1024]{2,1,0:T(8,128)(2,1)S(1)}, u32[]{:S(2)}, u32[]{:S(2)}) collective-permute-start(bf16[23,32,1024]{2,1,0:T(8,128)(2,1)S(1)} %gather.79), channel_id=1, source_target_pairs={{0,8},{4,12},{8,0},{12,4},{16,24},{20,28},{24,16},{28,20},{1,9},{5... | collective-permute-start | bytes 4521992 | tf_op jit(solution)/shard_map/cond/branch_1_fun/ppermute | solution.py:197
  166.9 13.9 %copy-start.7 = (bf16[1024,288]{1,0:T(8,128)(2,1)S(1)}, bf16[1024,288]{1,0:T(8,128)(2,1)}, u32[]{:S(2)}) copy-start(bf16[1024,288]{1,0:T(8,128)(2,1)} %copy-done.5) | copy-start | bytes 1769476 | tf_op jit(solution)/shard_map/cond
  196.9 3.4 %collective-permute-start.29 = (bf16[23,32,1024]{2,1,0:T(8,128)(2,1)S(1)}, bf16[23,32,1024]{2,1,0:T(8,128)(2,1)S(1)}, u32[]{:S(2)}, u32[]{:S(2)}) collective-permute-start(bf16[23,32,1024]{2,1,0:T(8,128)(2,1)S(1)} %gather.89), channel_id=1, source_target_pairs={{0,4},{4,0},{8,12},{12,8},{16,20},{20,16},{24,28},{28,24},{1,5},{5... | collective-permute-start | bytes 4521992 | tf_op jit(solution)/shard_map/cond/branch_1_fun/ppermute | solution.py:197
  199.4 13.9 %collective-permute-start.27 = (bf16[23,32,1024]{2,1,0:T(8,128)(2,1)S(1)}, bf16[23,32,1024]{2,1,0:T(8,128)(2,1)S(1)}, u32[]{:S(2)}, u32[]{:S(2)}) collective-permute-start(bf16[23,32,1024]{2,1,0:T(8,128)(2,1)S(1)} %gather.88), channel_id=1, source_target_pairs={{0,4},{4,0},{8,12},{12,8},{16,20},{20,16},{24,28},{28,24},{1,5},{5... | collective-permute-start | bytes 4521992 | tf_op jit(solution)/shard_map/cond/branch_1_fun/ppermute | solution.py:197
  (6 other events, 11.8 us)

commit v4 on v3

--- a/solution.py
+++ b/solution.py
@@ -415,21 +415,23 @@
                 one.hop()
             if n == 0:
                 kv.hop()
-            if following:
-                for one in following:
-                    one.collect()
-                flow_first, *sent = lax.optimization_barrier(
-                    (first, *(one.sent for one in following))
-                )
-                for one, rows in zip(following, sent):
-                    one.sent = rows
-                    one.travel()
             if n == 0:
-                kv_packed = pack(tables[0][3], flow_first, pick, *kv.got(), kv_local)
+                kv_packed = pack(tables[0][3], first, pick, *kv.got(), kv_local)
             for half, one in enumerate(rounds[n]):
                 out = attend_one(
                     half * per_half + n, kv_packed, flow_first, one.got(), tables[half][3], out
                 )
+                if following and half == 0:
+                    out, *held = lax.optimization_barrier((out, *(each.lists for each in following)))
+                    for each, lists in zip(following, held):
+                        each.lists = lists
+                        each.collect()
+                    flow_first, *sent = lax.optimization_barrier(
+                        (first, *(each.sent for each in following))
+                    )
+                    for each, rows in zip(following, sent):
+                        each.sent = rows
+                        each.travel()
             if following:
                 out, *held = lax.optimization_barrier((out, *(one.lists for one in following)))
                 for one, lists in zip(following, held):

time: 223 us -> 213 us (0.955); the launches traced: 227 us -> 212 us
  waiting for transfers between devices: 89.8 us -> 80.9 us
    all_to_all x1, waiting for transfers between devices: 17.5 us -> 0.01 us  [own_heads(): lax.all_to_all(jnp.transpose(kv, (2, 0, 1, 3)), 'tensor', split_axis=0, c...]
    ppermute x15, waiting for transfers between devices: 72.3 us -> 80.9 us  [flip(): return lax.ppermute(rows, 'dp', pairs)]
  transfers between devices with their start and end apart: 16 -> 16, of which waited for: 8 -> 8; matrix products, arithmetic and copies ran while one was open for 1% -> 1% of each run, Pallas kernels for 33% -> 34%
where the time goes in v4:
time: 213 us; the launch traced here: 212 us
  Pallas kernels  87.9 us (41%)
  waiting for transfers between devices  80.9 us (38%)
  starting transfers between devices  15.9 us (7%)
  blocking collectives  10.3 us (5%)
  other arithmetic  7.86 us (4%)
  between operations  4.29 us (2%)
  local copies, waits for them, and re-layouts  3.16 us (1%)
    ppermute x15, waiting for transfers between devices, flip(): return lax.ppermute(rows, 'dp', pairs)  80.9 us
    pallas_call x4, Pallas kernels, attend(): pl.pallas_call(functools.partial(attend_kernel, cols=cols, bases=bases, h...  52.2 us
    pallas_call x15, Pallas kernels, gather(): pl.pallas_call(functools.partial(gather_kernel, cols=cols, bases=bases),...  31 us
    ppermute x15, starting transfers between devices, flip(): return lax.ppermute(rows, 'dp', pairs)  11.1 us
    all_gather x1, blocking collectives, per_device(): table = lax.all_gather(jnp.stack([destination, token_count]), 'dp', axis=0)  10.3 us
    all_to_all x1, starting transfers between devices, own_heads(): lax.all_to_all(jnp.transpose(kv, (2, 0, 1, 3)), 'tensor', split_axis=0, c...  4.87 us
    pallas_call x1, Pallas kernels, pack(): pl.pallas_call(functools.partial(pack_kernel, cols=cols, bases=bases), gr...  4.59 us
  transfers between devices with their start and end apart: 16, of which 8 were waited for; matrix products, arithmetic and copies ran while one was open for 1% of the time, Pallas kernels for 34%

profile of v4, /device:TPU:0, one launch (start us, length us, event | category | flops | bytes accessed | tf_op | source)
XLA Modules:
  0.0 212.0 jit_solution(14165092212306316032)
XLA Ops:
  1.8 10.3 %all-gather.1 = s32[8,2,32]{2,1,0:T(2,128)S(1)} all-gather(s32[1,2,32]{2,1,0:T(2,128)S(1)} %add_bitcast_fusion), channel_id=2, replica_groups=mesh['dp'=8,'tensor'=4] {'dp'}, dimensions={0}, use_global_device_ids=true | all-gather | bytes 2304 | tf_op jit(solution)/shard_map/all_gather | solution.py:293
  24.1 187.8 %conditional.1 = (bf16[1024,4096]{1,0:T(8,128)(2,1)}) conditional(s32[]{:T(128)} %clamp.3, (pred[4,256]{1,0:T(4,128)(4,1)S(1)}, pred[4,256]{1,0:T(4,128)(4,1)S(1)}, bf16[8,32,1024]{2,1,0:T(8,128)(2,1)S(1)}, bf16[8,32,1024]{2,1,0:T(8,128)(2,1)S(1)}, s32[8]{0:T(128)S(1)}, /*index=5*/bf16[1024,288]{1,0:T(8,128)(2,1)S(1)}, ...), branch_computations={%region_19.20_spmd, %region_20.21_spmd, %region_21.22_spmd, %regio... | conditional | flops 6446379008 | bytes 285617600 | solution.py:443
  24.4 3.0 %gather.64 = bf16[21,32,1024]{2,1,0:T(8,128)(2,1)} custom-call(s32[21]{0:T(128)S(1)} %get-tuple-element.735.code_ref, bf16[32,32,4096]{2,1,0:T(8,128)(2,1)} %get-tuple-element.235.rest_0_), custom_call_target="tpu_custom_call" | custom-call | bytes 2752512 | tf_op jit(solution)/shard_map/cond/branch_0_fun/gather/pallas_call | solution.py:52
  27.4 1.6 collective-permute-start.4
  30.2 4.9 %all-to-all-start = ((bf16[4,8,32,512]{3,2,1,0:T(8,128)(2,1)}), bf16[4,8,32,512]{3,2,1,0:T(8,128)(2,1)S(1)}, u32[]{:S(2)}, u32[]{:S(2)}) async-start(bf16[4,8,32,512]{3,2,1,0:T(8,128)(2,1)} %maximum_bitcast_fusion), calls=%async_computation | async-start | bytes 2097152 | tf_op jit(solution)/shard_map/cond/branch_0_fun/all_to_all | solution.py:300
  35.2 3.0 %gather.70 = bf16[21,32,1024]{2,1,0:T(8,128)(2,1)} custom-call(s32[21]{0:T(128)S(1)} %get-tuple-element.732.code_ref, bf16[32,32,4096]{2,1,0:T(8,128)(2,1)} %get-tuple-element.235.rest_0_), custom_call_target="tpu_custom_call" | custom-call | bytes 2752512 | tf_op jit(solution)/shard_map/cond/branch_0_fun/gather/pallas_call | solution.py:52
  38.8 21.4 %collective-permute-done.4.rest_1_ = bf16[21,32,1024]{2,1,0:T(8,128)(2,1)} collective-permute-done((bf16[21,32,1024]{2,1,0:T(8,128)(2,1)}, bf16[21,32,1024]{2,1,0:T(8,128)(2,1)}, u32[]{:S(2)}, u32[]{:S(2)}) %collective-permute-start.4) | collective-permute-done | bytes 1376288 | tf_op jit(solution)/shard_map/cond/branch_0_fun/ppermute | solution.py:197
  60.2 3.0 %gather.65 = bf16[21,32,1024]{2,1,0:T(8,128)(2,1)} custom-call(s32[21]{0:T(128)S(1)} %get-tuple-element.734.code_ref, bf16[32,32,4096]{2,1,0:T(8,128)(2,1)} %get-tuple-element.235.rest_0_, bf16[21,32,1024]{2,1,0:T(8,128)(2,1)} %collective-permute-done.4.rest_1_), custom_call_target="tpu_custom_call" | custom-call | bytes 2752512 | tf_op jit(solution)/shard_map/cond/branch_0_fun/gather/pallas_call | solution.py:52
  63.2 1.5 collective-permute-start.5
  64.7 1.6 gather.60
  66.9 4.6 %collective-permute-done.9.rest_1_ = bf16[21,32,1024]{2,1,0:T(8,128)(2,1)S(1)} collective-permute-done((bf16[21,32,1024]{2,1,0:T(8,128)(2,1)}, bf16[21,32,1024]{2,1,0:T(8,128)(2,1)S(1)}, u32[]{:S(2)}, u32[]{:S(2)}) %collective-permute-start.9) | collective-permute-done | bytes 1376288 | tf_op jit(solution)/shard_map/cond/branch_0_fun/ppermute | solution.py:197
  71.6 2.6 %gather.71 = bf16[21,32,1024]{2,1,0:T(8,128)(2,1)S(1)} custom-call(s32[21]{0:T(128)S(1)} %get-tuple-element.731.code_ref, bf16[32,32,4096]{2,1,0:T(8,128)(2,1)} %get-tuple-element.235.rest_0_, bf16[21,32,1024]{2,1,0:T(8,128)(2,1)S(1)} %collective-permute-done.9.rest_1_), custom_call_target="tpu_custom_call" | custom-call | bytes 2752512 | tf_op jit(solution)/shard_map/cond/branch_0_fun/gather/pallas_call | solution.py:52
  74.6 10.2 %collective-permute-done.rest_1_ = bf16[21,32,512]{2,1,0:T(8,128)(2,1)S(1)} collective-permute-done((bf16[21,32,512]{2,1,0:T(8,128)(2,1)S(1)}, bf16[21,32,512]{2,1,0:T(8,128)(2,1)S(1)}, u32[]{:S(2)}, u32[]{:S(2)}) %collective-permute-start) | collective-permute-done | bytes 688160 | tf_op jit(solution)/shard_map/cond/branch_0_fun/ppermute | solution.py:197
  84.8 1.8 gather.61
  87.2 13.9 %collective-permute-done.5.rest_2_ = bf16[21,32,1024]{2,1,0:T(8,128)(2,1)} collective-permute-done((bf16[21,32,1024]{2,1,0:T(8,128)(2,1)}, bf16[21,32,1024]{2,1,0:T(8,128)(2,1)}, u32[]{:S(2)}, u32[]{:S(2)}) %collective-permute-start.5) | collective-permute-done | bytes 1376288 | tf_op jit(solution)/shard_map/cond/branch_0_fun/ppermute | solution.py:197
  101.2 1.8 gather.66
  106.2 1.5 collective-permute-start.7
  107.7 8.1 %collective-permute-done.1.rest_2_ = bf16[21,32,512]{2,1,0:T(8,128)(2,1)S(1)} collective-permute-done((bf16[21,32,512]{2,1,0:T(8,128)(2,1)S(1)}, bf16[21,32,512]{2,1,0:T(8,128)(2,1)S(1)}, u32[]{:S(2)}, u32[]{:S(2)}) %collective-permute-start.1) | collective-permute-done | bytes 688160 | tf_op jit(solution)/shard_map/cond/branch_0_fun/ppermute | solution.py:197
  115.8 1.9 gather.62
  118.2 2.1 gather.72
  121.1 4.6 %pack.4 = (bf16[2,1280,128]{2,1,0:T(8,128)(2,1)S(1)}, bf16[2,1280,128]{2,1,0:T(8,128)(2,1)S(1)}) custom-call(s32[32]{0:T(128)S(1)} %slice_bitcast_fusion.12.code_ref, s32[8]{0:T(128)S(1)} %get-tuple-element.90.first_ref, bf16[1024,288]{1,0:T(8,128)(2,1)S(1)} %get-tuple-element.77.pick_ref, bf16[32,32,512]{2,1,0:T(8,128)(2,1)S(1)} %bitcast.235, ...), custom_call_target="tpu_custom_call" | custom-call | tf_op jit(solution)/shard_map/cond/branch_0_fun/pack/pallas_call | solution.py:95
  125.7 12.2 %attend.16.rest_4_ = bf16[1024,4096]{1,0:T(8,128)(2,1)} custom-call(s32[32]{0:T(128)S(1)} %slice_bitcast_fusion.12.code_ref, s32[8]{0:T(128)S(1)} %get-tuple-element.90.first_ref, bf16[2,1280,128]{2,1,0:T(8,128)(2,1)S(1)} %get-tuple-element.81.k_ref, bf16[2,1280,128]{2,1,0:T(8,128)(2,1)S(1)} %get-tuple-element.82.v_ref, ...), custom_call_target="tpu_custom_call" | custom-call | flops 1610612736 | bytes 6291456 | tf_op jit(solution)/shard_map/cond/branch_0_fun/attend/pallas_call | solution.py:170
  137.9 6.6 %collective-permute-done.3.rest_1_ = bf16[21,32,1024]{2,1,0:T(8,128)(2,1)S(1)} collective-permute-done((bf16[21,32,1024]{2,1,0:T(8,128)(2,1)S(1)}, bf16[21,32,1024]{2,1,0:T(8,128)(2,1)S(1)}, u32[]{:S(2)}, u32[]{:S(2)}) %collective-permute-start.3) | collective-permute-done | bytes 1376288 | tf_op jit(solution)/shard_map/cond/branch_0_fun/ppermute | solution.py:197
  144.5 1.9 gather.69
  146.4 1.9 gather.68
  148.5 1.6 collective-permute-start.8
  150.1 13.4 %attend.17.rest_4_ = bf16[1024,4096]{1,0:T(8,128)(2,1)} custom-call(s32[32]{0:T(128)S(1)} %slice_bitcast_fusion.13.code_ref, s32[8]{0:T(128)S(1)} %get-tuple-element.90.first_ref, bf16[2,1280,128]{2,1,0:T(8,128)(2,1)S(1)} %get-tuple-element.81.k_ref, bf16[2,1280,128]{2,1,0:T(8,128)(2,1)S(1)} %get-tuple-element.82.v_ref, ...), custom_call_target="tpu_custom_call", output_to_operand_aliasing={{}: (10, {})} | custom-call | flops 1610612736 | bytes 6291456 | tf_op jit(solution)/shard_map/cond/branch_0_fun/attend/pallas_call | solution.py:170
  163.5 15.8 %collective-permute-done.13.rest_2_ = bf16[21,32,1024]{2,1,0:T(8,128)(2,1)S(1)} collective-permute-done((bf16[21,32,1024]{2,1,0:T(8,128)(2,1)S(1)}, bf16[21,32,1024]{2,1,0:T(8,128)(2,1)S(1)}, u32[]{:S(2)}, u32[]{:S(2)}) %collective-permute-start.13) | collective-permute-done | bytes 1376288 | tf_op jit(solution)/shard_map/cond/branch_0_fun/ppermute | solution.py:197
  179.3 2.1 gather.74
  181.5 2.1 gather.73
  184.6 13.3 %attend.18.rest_4_ = bf16[1024,4096]{1,0:T(8,128)(2,1)} custom-call(s32[32]{0:T(128)S(1)} %slice_bitcast_fusion.12.code_ref, s32[8]{0:T(128)S(1)} %get-tuple-element.90.first_ref, bf16[2,1280,128]{2,1,0:T(8,128)(2,1)S(1)} %get-tuple-element.81.k_ref, bf16[2,1280,128]{2,1,0:T(8,128)(2,1)S(1)} %get-tuple-element.82.v_ref, ...), custom_call_target="tpu_custom_call", output_to_operand_aliasing={{}: (10, {})} | custom-call | flops 1610612736 | bytes 6291456 | tf_op jit(solution)/shard_map/cond/branch_0_fun/attend/pallas_call | solution.py:170
  197.9 13.4 %attend.19 = bf16[1024,4096]{1,0:T(8,128)(2,1)} custom-call(s32[32]{0:T(128)S(1)} %slice_bitcast_fusion.13.code_ref, s32[8]{0:T(128)S(1)} %get-tuple-element.90.first_ref, bf16[2,1280,128]{2,1,0:T(8,128)(2,1)S(1)} %get-tuple-element.81.k_ref, bf16[2,1280,128]{2,1,0:T(8,128)(2,1)S(1)} %get-tuple-element.82.v_ref, ...), custom_call_target="tpu_custom_call", output_to_operand_aliasing={{}: (10, {})} | custom-call | flops 1610612736 | bytes 6291456 | tf_op jit(solution)/shard_map/cond/branch_0_fun/attend/pallas_call | solution.py:170
  (117 shorter events, 19.3 us)
Async XLA Ops:
  0.0 24.0 %copy-start.19 = (s32[1,1024]{1,0:T(1,128)S(1)}, s32[1,1024]{1,0:T(1,128)}, u32[]{:S(2)}) copy-start(s32[1,1024]{1,0:T(1,128)} %param.15) | copy-start | bytes 12292
  0.0 24.0 %copy-start.10 = (bf16[8,32,1024]{2,1,0:T(8,128)(2,1)S(1)}, bf16[8,32,1024]{2,1,0:T(8,128)(2,1)}, u32[]{:S(2)}) copy-start(bf16[8,32,1024]{2,1,0:T(8,128)(2,1)} %param.12) | copy-start | bytes 1572868
  0.0 24.0 %copy-start.5 = (bf16[8,32,1024]{2,1,0:T(8,128)(2,1)S(1)}, bf16[8,32,1024]{2,1,0:T(8,128)(2,1)}, u32[]{:S(2)}) copy-start(bf16[8,32,1024]{2,1,0:T(8,128)(2,1)} %param.11) | copy-start | bytes 1572868
  27.4 32.8 %collective-permute-start.4 = (bf16[21,32,1024]{2,1,0:T(8,128)(2,1)}, bf16[21,32,1024]{2,1,0:T(8,128)(2,1)}, u32[]{:S(2)}, u32[]{:S(2)}) collective-permute-start(bf16[21,32,1024]{2,1,0:T(8,128)(2,1)} %gather.64), channel_id=1, source_target_pairs={{0,8},{4,12},{8,0},{12,4},{16,24},{20,28},{24,16},{28,20},{1,9},{5... | collective-permute-start | bytes 4128776 | tf_op jit(solution)/shard_map/cond/branch_0_fun/ppermute | solution.py:197
  30.2 34.6 %all-to-all-start = ((bf16[4,8,32,512]{3,2,1,0:T(8,128)(2,1)}), bf16[4,8,32,512]{3,2,1,0:T(8,128)(2,1)S(1)}, u32[]{:S(2)}, u32[]{:S(2)}) async-start(bf16[4,8,32,512]{3,2,1,0:T(8,128)(2,1)} %maximum_bitcast_fusion), calls=%async_computation | async-start | bytes 2097152 | tf_op jit(solution)/shard_map/cond/branch_0_fun/all_to_all | solution.py:300
  38.2 33.3 %collective-permute-start.9 = (bf16[21,32,1024]{2,1,0:T(8,128)(2,1)}, bf16[21,32,1024]{2,1,0:T(8,128)(2,1)S(1)}, u32[]{:S(2)}, u32[]{:S(2)}) collective-permute-start(bf16[21,32,1024]{2,1,0:T(8,128)(2,1)} %gather.70), channel_id=1, source_target_pairs={{0,16},{4,20},{8,24},{12,28},{16,0},{20,4},{24,8},{28,12},{1,17},{... | collective-permute-start | bytes 4128776 | tf_op jit(solution)/shard_map/cond/branch_0_fun/ppermute | solution.py:197
  63.2 37.9 %collective-permute-start.5 = (bf16[21,32,1024]{2,1,0:T(8,128)(2,1)}, bf16[21,32,1024]{2,1,0:T(8,128)(2,1)}, u32[]{:S(2)}, u32[]{:S(2)}) collective-permute-start(bf16[21,32,1024]{2,1,0:T(8,128)(2,1)} %gather.65), channel_id=1, source_target_pairs={{0,16},{4,20},{8,24},{12,28},{16,0},{20,4},{24,8},{28,12},{1,17},{... | collective-permute-start | bytes 4128776 | tf_op jit(solution)/shard_map/cond/branch_0_fun/ppermute | solution.py:197
  64.7 36.4 %slice-start = ((s8[8388608]{0:T(1024)(128)(4,1)}), s8[4194304]{0:T(1024)(128)(4,1)S(1)}, s32[]{:S(2)}) async-start(s8[8388608]{0:T(1024)(128)(4,1)} %bitcast.248), calls=%async_computation.4 | async-start | bytes 8388608 | tf_op jit(solution)/shard_map/cond
  66.3 18.4 %collective-permute-start = (bf16[21,32,512]{2,1,0:T(8,128)(2,1)S(1)}, bf16[21,32,512]{2,1,0:T(8,128)(2,1)S(1)}, u32[]{:S(2)}, u32[]{:S(2)}) collective-permute-start(bf16[21,32,512]{2,1,0:T(8,128)(2,1)S(1)} %gather.60), channel_id=1, source_target_pairs={{0,8},{4,12},{8,0},{12,4},{16,24},{20,28},{24,16},{28,20},{1,9},{5... | collective-permute-start | bytes 2064392 | tf_op jit(solution)/shard_map/cond/branch_0_fun/ppermute | solution.py:197
  71.6 29.6 %slice-start.1 = ((s8[8388608]{0:T(1024)(128)(4,1)}), s8[4194304]{0:T(1024)(128)(4,1)S(1)}, s32[]{:S(2)}) async-start(s8[8388608]{0:T(1024)(128)(4,1)} %bitcast.248), calls=%async_computation.5 | async-start | bytes 8388608 | tf_op jit(solution)/shard_map/cond
  74.1 44.1 %collective-permute-start.10 = (bf16[21,32,1024]{2,1,0:T(8,128)(2,1)S(1)}, bf16[21,32,1024]{2,1,0:T(8,128)(2,1)S(1)}, u32[]{:S(2)}, u32[]{:S(2)}) collective-permute-start(bf16[21,32,1024]{2,1,0:T(8,128)(2,1)S(1)} %gather.71), channel_id=1, source_target_pairs={{0,8},{4,12},{8,0},{12,4},{16,24},{20,28},{24,16},{28,20},{1,9},{5... | collective-permute-start | bytes 4128776 | tf_op jit(solution)/shard_map/cond/branch_0_fun/ppermute | solution.py:197
  86.6 29.2 %collective-permute-start.1 = (bf16[21,32,512]{2,1,0:T(8,128)(2,1)S(1)}, bf16[21,32,512]{2,1,0:T(8,128)(2,1)S(1)}, u32[]{:S(2)}, u32[]{:S(2)}) collective-permute-start(bf16[21,32,512]{2,1,0:T(8,128)(2,1)S(1)} %gather.61), channel_id=1, source_target_pairs={{0,16},{4,20},{8,24},{12,28},{16,0},{20,4},{24,8},{28,12},{1,17},{... | collective-permute-start | bytes 2064392 | tf_op jit(solution)/shard_map/cond/branch_0_fun/ppermute | solution.py:197
  103.0 22.7 %collective-permute-start.6 = (bf16[21,32,1024]{2,1,0:T(8,128)(2,1)S(1)}, bf16[21,32,1024]{2,1,0:T(8,128)(2,1)S(1)}, u32[]{:S(2)}, u32[]{:S(2)}) collective-permute-start(bf16[21,32,1024]{2,1,0:T(8,128)(2,1)S(1)} %gather.66), channel_id=1, source_target_pairs={{0,4},{4,0},{8,12},{12,8},{16,20},{20,16},{24,28},{28,24},{1,5},{5... | collective-permute-start | bytes 4128776 | tf_op jit(solution)/shard_map/cond/branch_0_fun/ppermute | solution.py:197
  104.3 40.2 %collective-permute-start.3 = (bf16[21,32,1024]{2,1,0:T(8,128)(2,1)S(1)}, bf16[21,32,1024]{2,1,0:T(8,128)(2,1)S(1)}, u32[]{:S(2)}, u32[]{:S(2)}) collective-permute-start(bf16[21,32,1024]{2,1,0:T(8,128)(2,1)S(1)} %gather.63), channel_id=1, source_target_pairs={{0,16},{4,20},{8,24},{12,28},{16,0},{20,4},{24,8},{28,12},{1,17},{... | collective-permute-start | bytes 4128776 | tf_op jit(solution)/shard_map/cond/branch_0_fun/ppermute | solution.py:197
  106.2 11.6 %copy-start.15 = (s32[128,384]{1,0:T(8,128)S(1)}, s32[128,384]{1,0:T(8,128)}, u32[]{:S(2)}) copy-start(s32[128,384]{1,0:T(8,128)} %get-tuple-element.448) | copy-start | bytes 589828 | tf_op jit(solution)/shard_map/cond
  106.2 40.2 %collective-permute-start.7 = (bf16[21,32,1024]{2,1,0:T(8,128)(2,1)S(1)}, bf16[21,32,1024]{2,1,0:T(8,128)(2,1)S(1)}, u32[]{:S(2)}, u32[]{:S(2)}) collective-permute-start(bf16[21,32,1024]{2,1,0:T(8,128)(2,1)S(1)} %gather.67), channel_id=1, source_target_pairs={{0,8},{4,12},{8,0},{12,4},{16,24},{20,28},{24,16},{28,20},{1,9},{5... | collective-permute-start | bytes 4128776 | tf_op jit(solution)/shard_map/cond/branch_0_fun/ppermute | solution.py:197
  117.7 3.4 %collective-permute-start.2 = (bf16[21,32,512]{2,1,0:T(8,128)(2,1)S(1)}, bf16[21,32,512]{2,1,0:T(8,128)(2,1)S(1)}, u32[]{:S(2)}, u32[]{:S(2)}) collective-permute-start(bf16[21,32,512]{2,1,0:T(8,128)(2,1)S(1)} %gather.62), channel_id=1, source_target_pairs={{0,4},{4,0},{8,12},{12,8},{16,20},{20,16},{24,28},{28,24},{1,5},{5... | collective-permute-start | bytes 2064392 | tf_op jit(solution)/shard_map/cond/branch_0_fun/ppermute | solution.py:197
  120.3 29.8 %collective-permute-start.11 = (bf16[21,32,1024]{2,1,0:T(8,128)(2,1)S(1)}, bf16[21,32,1024]{2,1,0:T(8,128)(2,1)S(1)}, u32[]{:S(2)}, u32[]{:S(2)}) collective-permute-start(bf16[21,32,1024]{2,1,0:T(8,128)(2,1)S(1)} %gather.72), channel_id=1, source_target_pairs={{0,4},{4,0},{8,12},{12,8},{16,20},{20,16},{24,28},{28,24},{1,5},{5... | collective-permute-start | bytes 4128776 | tf_op jit(solution)/shard_map/cond/branch_0_fun/ppermute | solution.py:197
  148.3 31.0 %collective-permute-start.13 = (bf16[21,32,1024]{2,1,0:T(8,128)(2,1)S(1)}, bf16[21,32,1024]{2,1,0:T(8,128)(2,1)S(1)}, u32[]{:S(2)}, u32[]{:S(2)}) collective-permute-start(bf16[21,32,1024]{2,1,0:T(8,128)(2,1)S(1)} %gather.68), channel_id=1, source_target_pairs={{0,16},{4,20},{8,24},{12,28},{16,0},{20,4},{24,8},{28,12},{1,17},{... | collective-permute-start | bytes 4128776 | tf_op jit(solution)/shard_map/cond/branch_0_fun/ppermute | solution.py:197
  148.5 33.0 %collective-permute-start.8 = (bf16[21,32,1024]{2,1,0:T(8,128)(2,1)S(1)}, bf16[21,32,1024]{2,1,0:T(8,128)(2,1)S(1)}, u32[]{:S(2)}, u32[]{:S(2)}) collective-permute-start(bf16[21,32,1024]{2,1,0:T(8,128)(2,1)S(1)} %gather.69), channel_id=1, source_target_pairs={{0,8},{4,12},{8,0},{12,4},{16,24},{20,28},{24,16},{28,20},{1,9},{5... | collective-permute-start | bytes 4128776 | tf_op jit(solution)/shard_map/cond/branch_0_fun/ppermute | solution.py:197
  181.4 3.2 %collective-permute-start.14 = (bf16[21,32,1024]{2,1,0:T(8,128)(2,1)S(1)}, bf16[21,32,1024]{2,1,0:T(8,128)(2,1)S(1)}, u32[]{:S(2)}, u32[]{:S(2)}) collective-permute-start(bf16[21,32,1024]{2,1,0:T(8,128)(2,1)S(1)} %gather.74), channel_id=1, source_target_pairs={{0,4},{4,0},{8,12},{12,8},{16,20},{20,16},{24,28},{28,24},{1,5},{5... | collective-permute-start | bytes 4128776 | tf_op jit(solution)/shard_map/cond/branch_0_fun/ppermute | solution.py:197
  183.6 14.4 %collective-permute-start.12 = (bf16[21,32,1024]{2,1,0:T(8,128)(2,1)S(1)}, bf16[21,32,1024]{2,1,0:T(8,128)(2,1)S(1)}, u32[]{:S(2)}, u32[]{:S(2)}) collective-permute-start(bf16[21,32,1024]{2,1,0:T(8,128)(2,1)S(1)} %gather.73), channel_id=1, source_target_pairs={{0,4},{4,0},{8,12},{12,8},{16,20},{20,16},{24,28},{28,24},{1,5},{5... | collective-permute-start | bytes 4128776 | tf_op jit(solution)/shard_map/cond/branch_0_fun/ppermute | solution.py:197
